TPU v7x, 32 devices: a whole 2x2x4 slice. The times are simulated.
32 devices in a mesh: dp: 8 (over y, x, core), mp: 4 (over z).
Axes of the slice: x: 2, y: 2, z: 4, core: 2. Of those that a mesh axis runs over, the one named last changes fastest.
Arguments:
- x_in: bfloat16 [8192, 768], P(('dp', 'mp')), may hold values from -6 to 6
- enc_in: bfloat16 [4096, 768], P(('dp', 'mp')), may hold values from -6 to 6
- cotangent: bfloat16 [8192, 768], P(('dp', 'mp')), may hold values from -6 to 6
- dec_len: int32 [8], P('dp'), may hold values from 128 to 1024, as said below
- enc_len: int32 [8], P('dp'), may hold values from 64 to 512, as said below
- self_qkv: bfloat16 [768, 3, 768], P(None, None, 'mp'), may hold values from -0.109375 to 0.109375
- self_out: bfloat16 [768, 768], P('mp'), may hold values from -1.75 to 1.75
- cross_q: bfloat16 [768, 768], P(None, 'mp'), may hold values from -0.0546875 to 0.0546875
- cross_kv: bfloat16 [768, 2, 768], P(None, None, 'mp'), may hold values from -0.21875 to 0.21875
- cross_out: bfloat16 [768, 768], P('mp'), may hold values from -1.25 to 1.25
- ff_in: bfloat16 [768, 2, 2048], P(None, None, 'mp'), may hold values from -0.21875 to 0.21875
- ff_out: bfloat16 [2048, 768], P('mp'), may hold values from -0.1875 to 0.1875
- gains: bfloat16 [3, 768], replicated, may hold values from 0.5 to 1.5
- table: bfloat16 [32, 12], P(None, 'mp'), may hold values from -6 to 6
Outputs:
- layer_out: bfloat16 [8192, 768], P(('dp', 'mp'))
- input_grad: float32 [8192, 768], P(('dp', 'mp'))
- enc_grad: float32 [4096, 768], P(('dp', 'mp'))
- self_qkv_grad: float32 [768, 3, 768], P(None, None, 'mp')
- self_out_grad: float32 [768, 768], P('mp')
- cross_q_grad: float32 [768, 768], P(None, 'mp')
- cross_kv_grad: float32 [768, 2, 768], P(None, None, 'mp')
- cross_out_grad: float32 [768, 768], P('mp')
- ff_in_grad: float32 [768, 2, 2048], P(None, None, 'mp')
- ff_out_grad: float32 [2048, 768], P('mp')
- gains_grad: float32 [3, 768], replicated
- table_grad: float32 [32, 12], P(None, 'mp')
Inputs may be any that keep to these rules, and one draw needn't show every extreme that they name: dec_len[s] is the number of live decoder positions of sequence s; the sequences on one index of dp are of similar length; some sequence has exactly 1024. enc_len[s] is the number of live encoder positions of sequence s; some sequence has exactly 512.
All inputs are finite; a program needn't handle non-finite values.
Results may differ from a plain program's by a relative error of at most 0.035.
Values may be sent and summed in bfloat16 or wider, within the bound.
A program may use at most 192 MiB of HBM per device.

v0:
```python
import math

import jax
import jax.numpy as jnp
from jax import lax
from jax.sharding import PartitionSpec as P

NB = 32
MAXD = 128
LDEC = 1024
LENC = 512


NORM_EPS = 1e-06
MASK_FILL = -1000000000.0


def bucket_index(distance):
    half_count = NB // 2
    clipped = jnp.maximum(distance, 0)
    bucket_ids = jnp.minimum(clipped, half_count)
    for level_pos in range(1, half_count):
        threshold = math.ceil(half_count * (MAXD / half_count) ** (level_pos / half_count))
        bucket_ids = bucket_ids + (clipped >= threshold).astype(jnp.int32)
    return bucket_ids


def bucket_tiles(row_start, row_count, key_start, key_count, dtype):
    query_pos = row_start + lax.broadcasted_iota(jnp.int32, (row_count, key_count), 0)
    key_pos = key_start + lax.broadcasted_iota(jnp.int32, (row_count, key_count), 1)
    bucket_ids = bucket_index(query_pos - key_pos)
    levels = lax.broadcasted_iota(jnp.int32, (NB, row_count, key_count), 0)
    return (levels == bucket_ids[None]).astype(dtype)


def norm_forward(values, gain_row):
    inv_rms = lax.rsqrt(jnp.mean(values * values, axis=-1, keepdims=True) + NORM_EPS)
    return ((values * inv_rms * gain_row).astype(jnp.bfloat16), inv_rms)


def norm_backward(values, inv_rms, gain_row, upstream):
    scaled = upstream * gain_row
    grad_in = inv_rms * scaled - values * inv_rms**3 * jnp.mean(
        scaled * values, axis=-1, keepdims=True
    )
    grad_gain = jnp.sum(upstream * values * inv_rms, axis=0)
    return (grad_in, grad_gain)


def dot_first(left, right):
    return lax.dot_general(
        left, right, (((0,), (0,)), ((), ())), preferred_element_type=jnp.float32
    )


def dot_last(left, right):
    return lax.dot_general(
        left, right, (((1,), (1,)), ((), ())), preferred_element_type=jnp.float32
    )


def gelu_tanh(values):
    return jax.nn.gelu(values, approximate=True)


def gather_rows(normed):
    return lax.all_gather(normed, "mp", axis=0, tiled=True)


def gather_back(grad_rows):
    return lax.all_gather(grad_rows, "mp", axis=0, tiled=True)


def spread_rows(source, weight, rows_here):

    def product(row_start, row_count):
        return jnp.dot(source, weight, preferred_element_type=jnp.float32)

    return lax.psum_scatter(
        product(jnp.int32(0), rows_here * lax.axis_size("mp")),
        "mp",
        scatter_dimension=0,
        tiled=True,
    )


def spread_back(source, weight, rows_here):

    def product(row_start, row_count):
        return dot_last(source, weight)

    return lax.psum_scatter(
        product(jnp.int32(0), rows_here * lax.axis_size("mp")),
        "mp",
        scatter_dimension=0,
        tiled=True,
    )


def block_scores(block_q, key_rows, bias_block, allowed):
    scores = (
        jnp.einsum("qhd,khd->hqk", block_q, key_rows, preferred_element_type=jnp.float32)
        + bias_block
    )
    return jnp.where(allowed[None], scores, MASK_FILL)


def attention_forward(queries, key_rows, value_rows, bias_list, valid_fn):
    length = queries.shape[1]
    qblock = min(512, length)
    outputs = []
    totals = []
    for block_pos in range(length // qblock):
        row_start = block_pos * qblock
        block_q = queries[0, row_start : row_start + qblock]
        scores = block_scores(
            block_q, key_rows[0], bias_list[block_pos], valid_fn(0, row_start, qblock)
        )
        row_maximum_score = jnp.max(scores, axis=-1, keepdims=True)
        logsum = row_maximum_score + jnp.log(
            jnp.sum(jnp.exp(scores - row_maximum_score), axis=-1, keepdims=True)
        )
        weights_low = jnp.exp(scores - logsum).astype(jnp.bfloat16)
        attended = jnp.einsum(
            "hqk,khd->qhd", weights_low, value_rows[0], preferred_element_type=jnp.float32
        )
        outputs.append(attended.astype(jnp.bfloat16))
        totals.append(logsum)
    return (jnp.concatenate(outputs, axis=0), totals)


def attention_backward(
    queries, key_rows, value_rows, bias_list, valid_fn, totals, grad_out, keep_scores
):
    length = queries.shape[1]
    qblock = min(512, length)
    block_count = length // qblock
    grad_queries = []
    score_sums = [None] * block_count
    key_acc = jnp.zeros(key_rows.shape[1:], jnp.float32)
    value_running_total = jnp.zeros(value_rows.shape[1:], jnp.float32)
    for block_pos in range(block_count):
        row_start = block_pos * qblock
        block_q = queries[0, row_start : row_start + qblock]
        block_grad = grad_out[0, row_start : row_start + qblock]
        scores = block_scores(
            block_q, key_rows[0], bias_list[block_pos], valid_fn(0, row_start, qblock)
        )
        weights_full = jnp.exp(scores - totals[block_pos])
        weights_low = weights_full.astype(jnp.bfloat16)
        grad_weights = jnp.einsum(
            "qhd,khd->hqk", block_grad, value_rows[0], preferred_element_type=jnp.float32
        )
        row_inner = jnp.sum(weights_full * grad_weights, axis=-1, keepdims=True)
        grad_scores = (weights_full * (grad_weights - row_inner)).astype(jnp.bfloat16)
        grad_queries.append(
            jnp.einsum(
                "hqk,khd->qhd", grad_scores, key_rows[0], preferred_element_type=jnp.float32
            ).astype(jnp.bfloat16)
        )
        key_acc = key_acc + jnp.einsum(
            "hqk,qhd->khd", grad_scores, block_q, preferred_element_type=jnp.float32
        )
        value_running_total = value_running_total + jnp.einsum(
            "hqk,qhd->khd", weights_low, block_grad, preferred_element_type=jnp.float32
        )
        if keep_scores:
            score_part = grad_scores.astype(jnp.float32)
            score_sums[block_pos] = score_part
    grad_keys = key_acc.astype(jnp.bfloat16)
    grad_values = value_running_total.astype(jnp.bfloat16)
    return (jnp.concatenate(grad_queries, axis=0), grad_keys, grad_values, score_sums)


def local(
    x_in,
    enc_in,
    cotangent,
    dec_len,
    enc_len,
    self_qkv,
    self_out,
    cross_q,
    cross_kv,
    cross_out,
    ff_in,
    ff_out,
    gains,
    table,
):
    rows_here = x_in.shape[0]
    model_width = x_in.shape[1]
    seq_count = dec_len.shape[0]
    head_count = table.shape[1]
    head_cols = self_qkv.shape[2]
    head_size = head_cols // head_count
    hidden_cols = ff_in.shape[2]
    qblock = min(512, LDEC)
    key_block_span = min(256, LDEC)
    gain_rows = gains.astype(jnp.float32)
    resid_zero = x_in.astype(jnp.float32)
    qkv_matrix = self_qkv.reshape(model_width, 3 * head_cols)
    kv_matrix = cross_kv.reshape(model_width, 2 * head_cols)
    hidden_matrix = ff_in.reshape(model_width, 2 * hidden_cols)
    bias_blocks = []
    for block_pos in range(LDEC // qblock):
        pieces = []
        for key_pos in range(LDEC // key_block_span):
            indicator_matrix = bucket_tiles(
                block_pos * qblock, qblock, key_pos * key_block_span, key_block_span, jnp.bfloat16
            )
            pieces.append(
                jnp.einsum(
                    "dvj,dp->pvj", indicator_matrix, table, preferred_element_type=jnp.float32
                )
            )
        bias_blocks.append(jnp.concatenate(pieces, axis=2))
    zero_bias = [0.0] * (LDEC // qblock)

    def causal_valid(seq_pos, row_start, row_count):
        query_pos = row_start + lax.broadcasted_iota(jnp.int32, (row_count, LDEC), 0)
        key_pos = lax.broadcasted_iota(jnp.int32, (row_count, LDEC), 1)
        return (key_pos <= query_pos) & (key_pos < dec_len[seq_pos])

    def encoder_valid(seq_pos, row_start, row_count):
        key_pos = lax.broadcasted_iota(jnp.int32, (row_count, LENC), 1)
        return key_pos < enc_len[seq_pos]

    normed_one, inv_one = norm_forward(resid_zero, gain_rows[0])
    full_one = gather_rows(normed_one)
    qkv_one = jnp.dot(full_one, qkv_matrix, preferred_element_type=jnp.float32).astype(jnp.bfloat16)
    qkv_split = qkv_one.reshape(seq_count, LDEC, 3, head_count, head_size)
    query_one = qkv_split[:, :, 0]
    key_one = qkv_split[:, :, 1]
    value_one = qkv_split[:, :, 2]
    attended_one, totals_one = attention_forward(
        query_one, key_one, value_one, bias_blocks, causal_valid
    )
    attended_one = attended_one.reshape(seq_count * LDEC, head_cols)
    resid_one = resid_zero + spread_rows(attended_one, self_out, rows_here)
    normed_two, inv_two = norm_forward(resid_one, gain_rows[1])
    complete_second = gather_rows(normed_two)
    query_two = (
        jnp.dot(complete_second, cross_q, preferred_element_type=jnp.float32)
        .astype(jnp.bfloat16)
        .reshape(seq_count, LDEC, head_count, head_size)
    )
    enc_full = lax.all_gather(enc_in, "mp", axis=0, tiled=True)
    kv_two = (
        jnp.dot(enc_full, kv_matrix, preferred_element_type=jnp.float32)
        .astype(jnp.bfloat16)
        .reshape(seq_count, LENC, 2, head_count, head_size)
    )
    key_two = kv_two[:, :, 0]
    value_two = kv_two[:, :, 1]
    attended_two, totals_two = attention_forward(
        query_two, key_two, value_two, zero_bias, encoder_valid
    )
    attended_two = attended_two.reshape(seq_count * LDEC, head_cols)
    resid_two = resid_one + spread_rows(attended_two, cross_out, rows_here)
    normed_three, inv_three = norm_forward(resid_two, gain_rows[2])
    full_three = gather_rows(normed_three)
    gate_up = jnp.dot(full_three, hidden_matrix, preferred_element_type=jnp.float32)
    gate_part = gate_up[:, :hidden_cols]
    up_part = gate_up[:, hidden_cols:]
    gelu_value, gelu_cotangent_map = jax.vjp(gelu_tanh, gate_part)
    activated = (gelu_value * up_part).astype(jnp.bfloat16)
    layer_out = resid_two + spread_rows(activated, ff_out, rows_here)
    grad_three = cotangent.astype(jnp.float32)
    back_three = gather_back(grad_three.astype(jnp.bfloat16))
    ff_out_grad = dot_first(activated, back_three)
    grad_act = dot_last(back_three, ff_out)
    grad_gate = gelu_cotangent_map(grad_act * up_part)[0]
    grad_hidden = jnp.concatenate([grad_gate, grad_act * gelu_value], axis=1).astype(jnp.bfloat16)
    ff_in_grad = dot_first(full_three, grad_hidden).reshape(model_width, 2, hidden_cols)
    norm_part, gain_three = norm_backward(
        resid_two, inv_three, gain_rows[2], spread_back(grad_hidden, hidden_matrix, rows_here)
    )
    grad_two = grad_three + norm_part
    back_two = gather_back(grad_two.astype(jnp.bfloat16))
    cross_out_grad = dot_first(attended_two, back_two)
    grad_att_two = (
        dot_last(back_two, cross_out)
        .astype(jnp.bfloat16)
        .reshape(seq_count, LDEC, head_count, head_size)
    )
    grad_query_two, grad_key_two, grad_value_two, unused = attention_backward(
        query_two, key_two, value_two, zero_bias, encoder_valid, totals_two, grad_att_two, False
    )
    grad_query_two = grad_query_two.reshape(seq_count * LDEC, head_cols)
    grad_kv = jnp.stack([grad_key_two, grad_value_two], axis=1).reshape(
        seq_count * LENC, 2 * head_cols
    )
    cross_q_grad = dot_first(complete_second, grad_query_two)
    cross_kv_grad = dot_first(enc_full, grad_kv).reshape(model_width, 2, head_cols)
    enc_grad = lax.psum_scatter(dot_last(grad_kv, kv_matrix), "mp", scatter_dimension=0, tiled=True)
    norm_part, gain_two = norm_backward(
        resid_one, inv_two, gain_rows[1], spread_back(grad_query_two, cross_q, rows_here)
    )
    grad_one = grad_two + norm_part
    back_one = gather_back(grad_one.astype(jnp.bfloat16))
    self_out_grad = dot_first(attended_one, back_one)
    grad_att_one = (
        dot_last(back_one, self_out)
        .astype(jnp.bfloat16)
        .reshape(seq_count, LDEC, head_count, head_size)
    )
    grad_query_one, grad_key_one, grad_value_one, score_sums = attention_backward(
        query_one, key_one, value_one, bias_blocks, causal_valid, totals_one, grad_att_one, True
    )
    grad_qkv = jnp.stack([grad_query_one, grad_key_one, grad_value_one], axis=1).reshape(
        seq_count * LDEC, 3 * head_cols
    )
    self_qkv_grad = dot_first(full_one, grad_qkv).reshape(model_width, 3, head_cols)
    table_grad = jnp.zeros((table.shape[0], head_count), jnp.float32)
    for block_pos in range(LDEC // qblock):
        for key_pos in range(LDEC // key_block_span):
            indicator_matrix = bucket_tiles(
                block_pos * qblock, qblock, key_pos * key_block_span, key_block_span, jnp.float32
            )
            score_tile = score_sums[block_pos][
                :, :, key_pos * key_block_span : (key_pos + 1) * key_block_span
            ]
            table_grad = table_grad + jnp.einsum(
                "gfy,pfy->pg",
                score_tile,
                indicator_matrix,
                precision=lax.Precision.HIGHEST,
                preferred_element_type=jnp.float32,
            )
    norm_part, gain_one = norm_backward(
        resid_zero, inv_one, gain_rows[0], spread_back(grad_qkv, qkv_matrix, rows_here)
    )
    input_grad = grad_one + norm_part
    (
        self_qkv_grad,
        self_out_grad,
        cross_q_grad,
        cross_kv_grad,
        cross_out_grad,
        ff_in_grad,
        ff_out_grad,
        table_grad,
    ) = lax.psum(
        (
            self_qkv_grad,
            self_out_grad,
            cross_q_grad,
            cross_kv_grad,
            cross_out_grad,
            ff_in_grad,
            ff_out_grad,
            table_grad,
        ),
        "dp",
    )
    gains_grad = lax.psum(jnp.stack([gain_one, gain_two, gain_three]), ("dp", "mp"))
    return (
        layer_out.astype(jnp.bfloat16),
        input_grad,
        enc_grad,
        self_qkv_grad,
        self_out_grad,
        cross_q_grad,
        cross_kv_grad,
        cross_out_grad,
        ff_in_grad,
        ff_out_grad,
        gains_grad,
        table_grad,
    )


def solution(mesh):
    in_specs = (
        P(("dp", "mp"), None),
        P(("dp", "mp"), None),
        P(("dp", "mp"), None),
        P("dp"),
        P("dp"),
        P(None, None, "mp"),
        P("mp", None),
        P(None, "mp"),
        P(None, None, "mp"),
        P("mp", None),
        P(None, None, "mp"),
        P("mp", None),
        P(),
        P(None, "mp"),
    )
    out_specs = (
        P(("dp", "mp"), None),
        P(("dp", "mp"), None),
        P(("dp", "mp"), None),
        P(None, None, "mp"),
        P("mp", None),
        P(None, "mp"),
        P(None, None, "mp"),
        P("mp", None),
        P(None, None, "mp"),
        P("mp", None),
        P(),
        P(None, "mp"),
    )
    return jax.shard_map(local, mesh=mesh, in_specs=in_specs, out_specs=out_specs, check_vma=False)
```

profile of v0, /device:TPU:0, one launch (start us, length us, event | category | flops | bytes accessed | tf_op | source)
XLA Modules:
  0.0 903.6 jit_solution(2324097600538504131)
XLA Ops:
  17.5 6.0 convert_add_fusion.1
  71.6 62.8 %reduce-scatter.8.cloned.1.call-done = f32[256,768]{1,0:T(8,128)} async-done(((f32[1024,768]{1,0:T(8,128)}), f32[256,768]{1,0:T(8,128)}) %reduce-scatter.8.cloned.1.call-update) | async-done | bytes 786448 | tf_op jit(solution)/shard_map/reduce_scatter | solution.py:79
  137.9 24.4 %all_gather.22 = bf16[512,768]{1,0:T(8,128)(2,1)S(1)} all-gather(bf16[128,768]{1,0:T(8,128)(2,1)S(1)} %copy-done.76), channel_id=1, replica_groups=mesh['dp'=8,'mp'=4] {'mp'}, dimensions={0}, use_global_device_ids=true | all-gather | bytes 983040 | tf_op jit(solution)/shard_map/all_gather | solution.py:248
  162.8 17.9 %all-gather.9.cloned.1.call-done = bf16[1024,768]{1,0:T(8,128)(2,1)} async-done(((bf16[256,768]{1,0:T(8,128)(2,1)}), bf16[1024,768]{1,0:T(8,128)(2,1)}) %all-gather.9.cloned.1.call-update) | async-done | bytes 1572880 | tf_op jit(solution)/shard_map/all_gather | solution.py:67
  191.9 60.2 %reduce-scatter.10.cloned.1.call-done = f32[256,768]{1,0:T(8,128)} async-done(((f32[1024,768]{1,0:T(8,128)}), f32[256,768]{1,0:T(8,128)}) %reduce-scatter.10.cloned.1.call-update) | async-done | bytes 786448 | tf_op jit(solution)/shard_map/reduce_scatter | solution.py:79
  258.8 33.3 %all-gather.11.cloned.1.call-done = bf16[1024,768]{1,0:T(8,128)(2,1)} async-done(((bf16[256,768]{1,0:T(8,128)(2,1)}), bf16[1024,768]{1,0:T(8,128)(2,1)}) %all-gather.11.cloned.1.call-update) | async-done | bytes 1572880 | tf_op jit(solution)/shard_map/all_gather | solution.py:67
  292.1 5.8 fusion.305
  297.9 31.6 %all-gather.13.cloned.1.call-done = bf16[1024,768]{1,0:T(8,128)(2,1)} async-done(((bf16[256,768]{1,0:T(8,128)(2,1)}), bf16[1024,768]{1,0:T(8,128)(2,1)}) %all-gather.13.cloned.1.call-update) | async-done | bytes 1572880 | tf_op jit(solution)/shard_map/all_gather | solution.py:71
  329.5 6.4 fusion.42
  337.2 3.5 fusion.50
  340.8 4.1 fusion.306
  345.0 55.1 %reduce-scatter.14.cloned.1.call-done = f32[256,768]{1,0:T(8,128)} async-done(((f32[1024,768]{1,0:T(8,128)}), f32[256,768]{1,0:T(8,128)}) %reduce-scatter.14.cloned.1.call-update) | async-done | bytes 786448 | tf_op jit(solution)/shard_map/reduce_scatter | solution.py:92
  402.6 60.1 %reduce-scatter.12.cloned.1.call-done = f32[256,768]{1,0:T(8,128)} async-done(((f32[1024,768]{1,0:T(8,128)}), f32[256,768]{1,0:T(8,128)}) %reduce-scatter.12.cloned.1.call-update) | async-done | bytes 786448 | tf_op jit(solution)/shard_map/reduce_scatter | solution.py:79
  465.6 37.2 %all-gather.15.cloned.1.call-done = bf16[1024,768]{1,0:T(8,128)(2,1)} async-done(((bf16[256,768]{1,0:T(8,128)(2,1)}), bf16[1024,768]{1,0:T(8,128)(2,1)}) %all-gather.15.cloned.1.call-update) | async-done | bytes 1572880 | tf_op jit(solution)/shard_map/all_gather | solution.py:71
  516.6 59.0 %reduce-scatter.16.cloned.1.call-done = f32[256,768]{1,0:T(8,128)} async-done(((f32[1024,768]{1,0:T(8,128)}), f32[256,768]{1,0:T(8,128)}) %reduce-scatter.16.cloned.1.call-update) | async-done | bytes 786448 | tf_op jit(solution)/shard_map/reduce_scatter | solution.py:92
  580.3 37.2 %all-gather.17.cloned.1.call-done = bf16[1024,768]{1,0:T(8,128)(2,1)} async-done(((bf16[256,768]{1,0:T(8,128)(2,1)}), bf16[1024,768]{1,0:T(8,128)(2,1)}) %all-gather.17.cloned.1.call-update) | async-done | bytes 1572880 | tf_op jit(solution)/shard_map/all_gather | solution.py:71
  619.6 4.1 fusion.92
  623.7 3.9 multiply_reduce_fusion
  650.9 5.1 fusion.49
  656.0 6.0 reshape.765
  662.1 3.7 fusion.313
  701.7 14.0 %psum.71 = f32[32,3]{0,1:T(4,128)} all-reduce(f32[32,3]{0,1:T(4,128)S(1)} %fusion.75), channel_id=1, replica_groups=mesh['dp'=8,'mp'=4] {'dp'}, use_global_device_ids=true, to_apply=%region_36.37 | all-reduce | flops 96 | bytes 768 | tf_op jit(solution)/shard_map/psum | solution.py:344
  717.2 40.2 %psum.70 = f32[3,768]{1,0:T(4,128)} all-reduce(f32[3,768]{1,0:T(4,128)S(1)} %pad_maximum_fusion.8), channel_id=1, replica_groups=mesh['dp'=8,'mp'=4] {'dp','mp'}, use_global_device_ids=true, to_apply=%region_35.36 | all-reduce | flops 2304 | bytes 18432 | tf_op jit(solution)/shard_map/psum | solution.py:357
  759.6 127.1 %all-reduce.3.cloned.1.call-done = (f32[768,3,192]{0,2,1:T(8,128)}, f32[192,768]{1,0:T(8,128)}, f32[768,192]{0,1:T(8,128)}, f32[768,2,192]{0,2,1:T(8,128)}, f32[...) async-done(((f32[768,3,192]{0,2,1:T(8,128)}, f32[192,768]{1,0:T(8,128)}, f32[768,192]{0,1:T(8,128)}, f32[768,2,192]{0,2,1:T(8,128)}, ...) | async-done | bytes 9437200 | tf_op jit(solution)/shard_map/psum | solution.py:344
  (372 shorter events, 178.2 us)
Async XLA Ops:
  7.2 45.6 %all-gather.7.cloned.1.call-start = ((), (), s32[]{:S(2)}) async-start(), calls=%async_computation.7 | async-start | bytes 1966080 | tf_op jit(solution)/shard_map/all_gather | solution.py:67
  10.4 125.9 %copy-start.88 = (f32[768]{0:T(1024)}, f32[768]{0:T(1024)S(1)}, u32[]{:S(2)}) copy-start(f32[768]{0:T(1024)S(1)} %get-tuple-element.19) | copy-start | bytes 9220
  12.9 121.5 %reduce-scatter.8.cloned.1.call-start = ((), (), s32[]{:S(2)}) async-start(), calls=%async_computation.8 | async-start | bytes 3932160 | tf_op jit(solution)/shard_map/reduce_scatter | solution.py:79
  69.2 65.2 %copy-start.13 = (bf16[256,768]{1,0:T(8,128)(2,1)S(1)}, bf16[256,768]{1,0:T(8,128)(2,1)}, u32[]{:S(2)}) copy-start(bf16[256,768]{1,0:T(8,128)(2,1)} %param.14) | copy-start | bytes 1179652
  71.5 66.4 %copy-start.76 = (bf16[128,768]{1,0:T(8,128)(2,1)S(1)}, bf16[128,768]{1,0:T(8,128)(2,1)}, u32[]{:S(2)}) copy-start(bf16[128,768]{1,0:T(8,128)(2,1)} %param.15) | copy-start | bytes 589828
  71.5 90.8 %copy-start.51 = (bf16[768,2,192]{0,2,1:T(8,128)(2,1)S(1)}, bf16[768,2,192]{0,2,1:T(8,128)(2,1)}, u32[]{:S(2)}) copy-start(bf16[768,2,192]{0,2,1:T(8,128)(2,1)} %param.22) | copy-start | bytes 1769476
  71.5 109.2 %all-gather.9.cloned.1.call-start = ((), (), s32[]{:S(2)}) async-start(), calls=%async_computation.9 | async-start | bytes 1966080 | tf_op jit(solution)/shard_map/all_gather | solution.py:67
  137.2 114.8 %reduce-scatter.10.cloned.1.call-start = ((), (), s32[]{:S(2)}) async-start(), calls=%async_computation.10 | async-start | bytes 3932160 | tf_op jit(solution)/shard_map/reduce_scatter | solution.py:79
  162.8 342.8 %copy-start.23 = (bf16[512,384]{0,1:T(8,128)(2,1)}, bf16[512,384]{0,1:T(8,128)(2,1)S(1)}, u32[]{:S(2)}) copy-start(bf16[512,384]{0,1:T(8,128)(2,1)S(1)} %convolution_convert_fusion.4) | copy-start | bytes 1179652
  191.8 62.2 %copy-start.87 = (f32[768]{0:T(1024)S(1)}, f32[768]{0:T(1024)}, u32[]{:S(2)}) copy-start(f32[768]{0:T(1024)} %get-tuple-element.18) | copy-start | bytes 9220
  191.8 100.3 %all-gather.11.cloned.1.call-start = ((), (), s32[]{:S(2)}) async-start(), calls=%async_computation.11 | async-start | bytes 1966080 | tf_op jit(solution)/shard_map/all_gather | solution.py:67
  254.8 74.7 %all-gather.13.cloned.1.call-start = ((), (), s32[]{:S(2)}) async-start(), calls=%async_computation.13 | async-start | bytes 1966080 | tf_op jit(solution)/shard_map/all_gather | solution.py:71
  255.4 144.6 %reduce-scatter.14.cloned.1.call-start = ((), (), s32[]{:S(2)}) async-start(), calls=%async_computation.14 | async-start | bytes 3932160 | tf_op jit(solution)/shard_map/reduce_scatter | solution.py:92
  340.8 121.9 %reduce-scatter.12.cloned.1.call-start = ((), (), s32[]{:S(2)}) async-start(), calls=%async_computation.12 | async-start | bytes 3932160 | tf_op jit(solution)/shard_map/reduce_scatter | solution.py:79
  344.9 117.8 %copy-start.46 = (bf16[256,768]{1,0:T(8,128)(2,1)S(1)}, bf16[256,768]{1,0:T(8,128)(2,1)}, u32[]{:S(2)}) copy-start(bf16[256,768]{1,0:T(8,128)(2,1)} %param.16) | copy-start | bytes 1179652
  344.9 157.9 %all-gather.15.cloned.1.call-start = ((), (), s32[]{:S(2)}) async-start(), calls=%async_computation.15 | async-start | bytes 1966080 | tf_op jit(solution)/shard_map/all_gather | solution.py:71
  465.5 110.1 %reduce-scatter.16.cloned.1.call-start = ((), (), s32[]{:S(2)}) async-start(), calls=%async_computation.16 | async-start | bytes 3932160 | tf_op jit(solution)/shard_map/reduce_scatter | solution.py:92
  516.3 101.2 %copy-start.75 = (bf16[192,768]{1,0:T(8,128)(2,1)S(1)}, bf16[192,768]{1,0:T(8,128)(2,1)}, u32[]{:S(2)}) copy-start(bf16[192,768]{1,0:T(8,128)(2,1)} %param.20) | copy-start | bytes 884740
  516.4 101.1 %all-gather.17.cloned.1.call-start = ((), (), s32[]{:S(2)}) async-start(), calls=%async_computation.17 | async-start | bytes 1966080 | tf_op jit(solution)/shard_map/all_gather | solution.py:71
  580.2 135.5 %reduce-scatter.18.cloned.1.call-start = ((), (), s32[]{:S(2)}) async-start(), calls=%async_computation.18 | async-start | bytes 3932160 | tf_op jit(solution)/shard_map/reduce_scatter | solution.py:92
  643.0 116.6 %reduce-scatter.20.cloned.1.call-start = ((), (), s32[]{:S(2)}) async-start(), calls=%async_computation.19 | async-start | bytes 1966080 | tf_op jit(solution)/shard_map/reduce_scatter | solution.py:296
  650.8 235.9 %all-reduce.3.cloned.1.call-start = ((), (), s32[]{:S(2)}) async-start(), calls=%async_computation.20 | async-start | bytes 18874368 | tf_op jit(solution)/shard_map/psum | solution.py:344
  698.8 58.6 %copy-start.28 = (f32[256,768]{1,0:T(8,128)S(1)}, f32[256,768]{1,0:T(8,128)}, u32[]{:S(2)}) copy-start(f32[256,768]{1,0:T(8,128)} %get-tuple-element.33) | copy-start | bytes 2359300
  698.8 58.6 %copy-start.100 = (f32[256]{0:T(256)S(1)}, f32[256]{0:T(256)}, u32[]{:S(2)}) copy-start(f32[256]{0:T(256)} %get-tuple-element.59) | copy-start | bytes 3076
  (100 other events, 720.5 us)
Sparse Core Ops, SparseCore 0:
  13.0 39.7 all-gather.6
  71.7 62.7 reduce-scatter.7
  137.3 43.3 all-gather.8
  191.9 60.0 reduce-scatter.9
  255.0 37.1 all-gather.10
  293.6 35.9 all-gather.12
  340.9 59.1 reduce-scatter.13
  402.4 60.2 reduce-scatter.11
  465.7 37.0 all-gather.14
  516.5 59.1 reduce-scatter.15
  580.4 37.0 all-gather.16
  643.1 59.1 reduce-scatter.17
  705.7 35.7 reduce-scatter.19
  746.8 139.8 all-reduce.2
where the time goes:
time: 913 us; the launch traced here: 904 us
  waiting for transfers between devices  583 us (64%)
  matrix products  137 us (15%)
  blocking collectives  78.6 us (9%)
  local copies, waits for them, and re-layouts  48.2 us (5%)
  other arithmetic  39.2 us (4%)
  between operations  16.7 us (2%)
    reduce_scatter x3, waiting for transfers between devices, spread_rows(): lax.psum_scatter(product(jnp.int32(0), rows_here * lax.axis_size('mp')),...  183 us
    psum x1, waiting for transfers between devices, local(): lax.psum((self_qkv_grad, self_out_grad, cross_q_grad, cross_kv_grad, cros...  127 us
    reduce_scatter x3, waiting for transfers between devices, spread_back(): lax.psum_scatter(product(jnp.int32(0), rows_here * lax.axis_size('mp')),...  114 us
    all_gather x3, waiting for transfers between devices, gather_back(): return lax.all_gather(grad_rows, 'mp', axis=0, tiled=True)  106 us
    all_gather x3, waiting for transfers between devices, gather_rows(): return lax.all_gather(normed, 'mp', axis=0, tiled=True)  51.4 us
    psum x1, blocking collectives, local(): lax.psum(jnp.stack([gain_one, gain_two, gain_three]), ('dp', 'mp'))  40.2 us
    unnamed x228, local copies, waits for them, and re-layouts  28.4 us
    all_gather x1, blocking collectives, local(): enc_full = lax.all_gather(enc_in, 'mp', axis=0, tiled=True)  24.4 us
  transfers between devices with their start and end apart: 14, of which 12 were waited for; matrix products, arithmetic and copies ran while one was open for 13% of the time, Pallas kernels for 0%

commit v1 on v0

v1 whole, which is shorter than its diff:
```python
import math

import jax
import jax.numpy as jnp
from jax import lax
from jax.experimental import pallas as pl
from jax.experimental.pallas import tpu as pltpu
from jax.sharding import PartitionSpec as P

NB = 32
MAXD = 128
NORM_EPS = 1e-06
MASK_FILL = -1000000000.0
MESH = pl.DeviceIdType.MESH
BF = jnp.bfloat16
F32 = jnp.float32
PARTS = 2
PADH = 16
GELU_C = math.sqrt(2.0 / math.pi)
SEMS = 224


def bucket_index(distance):
    half_count = NB // 2
    clipped = jnp.maximum(distance, 0)
    bucket_ids = jnp.minimum(clipped, half_count)
    for level_pos in range(1, half_count):
        threshold = math.ceil(half_count * (MAXD / half_count) ** (level_pos / half_count))
        bucket_ids = bucket_ids + (clipped >= threshold).astype(jnp.int32)
    return bucket_ids


def dot_nn(a, b):
    return lax.dot_general(a, b, (((1,), (0,)), ((), ())), preferred_element_type=F32)


def dot_nt(a, b):
    return lax.dot_general(a, b, (((1,), (1,)), ((), ())), preferred_element_type=F32)


def dot_tn(a, b):
    return lax.dot_general(a, b, (((0,), (0,)), ((), ())), preferred_element_type=F32)


def norm_fwd(v, g):
    inv = lax.rsqrt(jnp.mean(v * v, axis=-1, keepdims=True) + NORM_EPS)
    return (v * inv * g).astype(BF)


def norm_bwd(v, g, u):
    inv = lax.rsqrt(jnp.mean(v * v, axis=-1, keepdims=True) + NORM_EPS)
    gu = u * g
    mean = jnp.mean(gu * v, axis=-1, keepdims=True)
    grad = inv * gu - v * (inv * inv * inv * mean)
    gain = jnp.sum(u * v * inv, axis=0, keepdims=True)
    return grad, gain


class Dims:
    pass


def make_dims(mesh, x_in, enc_in, self_qkv, ff_in, table):
    d = Dims()
    d.ndp, d.nmp = mesh.shape["dp"], mesh.shape["mp"]
    d.nd = min(4, d.ndp // 2)
    d.R, d.D = x_in.shape
    d.E = enc_in.shape[0]
    d.nh = table.shape[1]
    d.hc = self_qkv.shape[2]
    d.hd = d.hc // d.nh
    d.F = ff_in.shape[2]
    d.ha = d.hd + PADH
    d.ne = 4 * d.E // d.R
    d.axr = -(-(2 + 2 * d.nh) // 8) * 8
    hc, F = d.hc, d.F
    names = (("qkv", 3 * hc), ("so", hc), ("cq", hc), ("ckv", 2 * hc), ("co", hc), ("gu", 2 * F), ("fo", F))
    d.w, at = {}, 0
    for name, rows in names:
        d.w[name] = (at, rows)
        at += rows
    d.rows = at
    s, c = 4 * hc, 4 * hc
    d.groups = {}
    land = 0
    for name, base, rows, loc in (("S", 0, s, 0), ("C", s, c, s), ("F", s + c, 3 * F, 0)):
        d.groups[name] = (base, rows, loc, land)
        land += rows // d.nd
    d.land = land
    d.locrows = max(s + c, 3 * F)
    d.small = -(-(3 + 4 * d.nh) // 8) * 8
    return d


def scratch_list(d):
    R, D, hc, nh, hd, ha, F, E = d.R, d.D, d.hc, d.nh, d.hd, d.ha, d.F, d.E
    full = ((4, R, D), BF)
    return [
        ("xb", (R, D), BF), ("cotb", (R, D), BF), ("aux", (d.axr, 4 * R), F32), ("wv", (d.rows, D), BF),
        ("h1f",) + full, ("h2f",) + full, ("h3f",) + full, ("d3f",) + full, ("d2f",) + full, ("d1f",) + full,
        ("encf", (4, E, D), BF),
        ("qa", (4, nh, ha, R), BF), ("ka", (4, nh, ha, R), BF), ("vT", (4, hc, R), BF), ("o1", (4, hc, R), BF),
        ("q2a", (4, nh, ha, R), BF), ("k2a", (d.ne, nh, ha, R), BF), ("v2T", (d.ne, hc, R), BF), ("o2", (4, hc, R), BF),
        ("lse1", (4, 8, R), F32), ("lse2", (4, 8, R), F32),
        ("bias", (nh, 3, R, R), F32), ("dsacc", (nh, 3, R, R), F32),
        ("x1", (R, D), F32), ("x2", (R, D), F32), ("gb", (R, D), F32),
        ("pb", (R, D), F32), ("sb", (3, R, D), BF), ("rb", (3, R, D), BF),
        ("opb", (R, D), F32), ("osb", (3, R, D), BF), ("orb", (3, R, D), BF), ("lov", (R, D), BF), ("igv", (R, D), BF),
        ("epb", (E, D), F32), ("esb", (3, E, D), BF), ("erb", (3, E, D), BF), ("egv", (E, D), BF),
        ("actT", (4, F, R), BF), ("dguT", (4, 2 * F, R), BF),
        ("da", (hc, R), BF), ("dqkvT", (4, 3 * hc, R), BF), ("dq2T", (4, hc, R), BF), ("dkv2T", (4, 2 * hc, E), BF),
        ("dka", (4, nh, ha, R), F32), ("dva", (4, hc, R), F32),
        ("gf", (d.locrows, D), F32), ("gsend", (d.rows, D), BF), ("grecv", (max(d.nd - 1, 1), d.land, D), BF),
        ("gz", (d.land, D), BF), ("gk", (d.land, D), F32), ("gfo", (d.land, D), BF),
        ("smc", (d.small, D), F32), ("sms", (6, d.small, D), F32), ("smr", (5, d.small, D), F32),
    ]


def build_kernel(d):
    R, D, hc, nh, hd, ha, F, E = d.R, d.D, d.hc, d.nh, d.hd, d.ha, d.F, d.E
    names = [item[0] for item in scratch_list(d)]
    wnames = list(d.w)
    HR = R // PARTS

    def kernel(*refs):
        x_ref, e_ref, cot_ref, aux_ref, gains_ref = refs[:5]
        w_refs = dict(zip(wnames, refs[5 : 5 + len(wnames)]))
        lo_ref, ig_ref, eg_ref, gout_ref, sm_ref = refs[5 + len(wnames) : 10 + len(wnames)]
        tail = refs[10 + len(wnames) :]
        v = Dims()
        for name, ref in zip(names, tail):
            setattr(v, name, ref)
        ss, rs, ls = tail[len(names) :]

        dp, z = lax.axis_index("dp"), lax.axis_index("mp")
        c, chip = dp % 2, dp // 2
        a, u = z % 2, z // 2
        t = a + 2 * c
        sw = c + u - 2 * c * u
        dl = chip % d.nd
        base_dp = (chip - dl) * 2
        sib = (dp + 1 - 2 * c, z)
        zp = (dp, z + 1 - 2 * a)
        z2 = (dp, z + 2 - 4 * u)
        mate = (2 * chip + u, a + 2 * c)
        d0, d1 = dl % 2, dl // 2
        flips = [dl, dl + 1 - 2 * d0, dl + 2 - 4 * d1, 3 - dl][: d.nd]
        peers = [(base_dp + 2 * f + c, z) for f in flips]
        is_sw, not_sw = sw == 1, sw == 0

        count = [0]

        def new_id():
            count[0] += 1
            assert count[0] <= SEMS
            return count[0] - 1

        class Xfer:
            def __init__(self, src, dst, dev):
                self.i, self.src, self.dst, self.dev = new_id(), src, dst, dev

            def desc(self):
                return pltpu.make_async_remote_copy(
                    src_ref=self.src, dst_ref=self.dst, send_sem=ss.at[self.i], recv_sem=rs.at[self.i],
                    device_id={"dp": self.dev[0], "mp": self.dev[1]}, device_id_type=MESH,
                )

            def start(self):
                self.desc().start()

            def recv(self):
                self.desc().wait_recv()

            def sent(self):
                self.desc().wait_send()

        class Local:
            def __init__(self, src, dst):
                self.i, self.src, self.dst = new_id(), src, dst

            def desc(self):
                return pltpu.make_async_copy(self.src, self.dst, ls.at[self.i])

            def start(self):
                self.desc().start()

            def wait(self):
                self.desc().wait()

        class Swap:
            def __init__(self, src, dst):
                self.far, self.near = Xfer(src, dst, mate), Local(src, dst)

            def start(self):
                pl.when(is_sw)(self.far.start)
                pl.when(not_sw)(self.near.start)

            def wait(self):
                pl.when(is_sw)(self.far.recv)
                pl.when(not_sw)(self.near.wait)

            def sent(self):
                pl.when(is_sw)(self.far.sent)

        class Weight:
            def __init__(self, name):
                first, rows = d.w[name]
                sl = rows // d.nd
                mine = pl.ds(pl.multiple_of(dl * sl, 16), sl)
                here = v.wv.at[pl.ds(pl.multiple_of(first + dl * sl, 16), sl)]
                self.near = Local(w_refs[name], v.wv.at[pl.ds(first, rows)])
                self.far = Xfer(w_refs[name].at[mine], here, mate)
                self.on = [Xfer(here, here, peer) for peer in peers[1:]]

            def start(self):
                pl.when(is_sw)(self.far.start)
                pl.when(not_sw)(self.near.start)

            def forward(self):
                @pl.when(is_sw)
                def _():
                    self.far.recv()
                    for x in self.on:
                        x.start()

            def wait(self):
                pl.when(not_sw)(self.near.wait)

                @pl.when(is_sw)
                def _():
                    for x in self.on:
                        x.recv()

            def sent(self):
                @pl.when(is_sw)
                def _():
                    self.far.sent()
                    for x in self.on:
                        x.sent()

        def blk_ag(k):
            k1, k2 = k % 2, k // 2
            return (a + k2 - 2 * a * k2) + 2 * (c + k1 - 2 * c * k1)

        def blk_rs(k):
            return blk_ag(3 - k)

        class Gather:
            def __init__(self, full, rows, parts):
                self.parts = parts
                n = rows // parts
                at = lambda b, h: full.at[b, pl.ds(h * n, n)]
                b_zp = (1 - a) + 2 * c
                self.z = [Xfer(at(t, h), at(t, h), zp) for h in range(parts)]
                self.c = [Xfer(at(t, h), at(t, h), sib) for h in range(parts)]
                self.f = [Xfer(at(b_zp, h), at(b_zp, h), sib) for h in range(parts)]

            def send(self, h):
                self.z[h].start()
                self.c[h].start()

            def near(self):
                for x in self.c:
                    x.recv()

            def far(self):
                for x, y in zip(self.z, self.f):
                    x.recv()
                    y.start()

            def last(self):
                for x in self.f:
                    x.recv()

            def arrive(self, k):
                pl.when(k == 1)(self.near)
                pl.when(k == 2)(self.far)
                pl.when(k == 3)(self.last)

            def sent(self):
                for x in self.z + self.c + self.f:
                    x.sent()

        class Scatter:
            def __init__(self, pb, sb, rb, rows, parts):
                self.pb, self.sb, self.rb, self.parts, self.n = pb, sb, rb, parts, rows // parts
                at = lambda r, i, h: r.at[i, pl.ds(h * self.n, self.n)]
                self.c0 = Xfer(sb.at[0], rb.at[0], sib)
                self.z = [Xfer(at(sb, 1, h), at(rb, 1, h), zp) for h in range(parts)]
                self.c2 = Xfer(sb.at[2], rb.at[2], sib)

            def emit(self, k):
                @pl.when(k == 0)
                def _():
                    self.sb[0] = self.pb[...].astype(BF)
                    self.c0.start()

                @pl.when(k == 1)
                def _():
                    self.c0.recv()
                    for h in range(self.parts):
                        rows = pl.ds(h * self.n, self.n)
                        self.sb[1, rows] = (self.pb[rows] + self.rb[0, rows].astype(F32)).astype(BF)
                        self.z[h].start()

                @pl.when(k == 2)
                def _():
                    self.sb[2] = self.pb[...].astype(BF)
                    self.c2.start()

            def loop(self, partial):
                def step(k, carry):
                    partial(blk_rs(k))
                    self.emit(k)
                    return carry

                lax.fori_loop(0, 4, step, 0)

            def finish(self, fin):
                self.c2.recv()
                for h in range(self.parts):
                    rows = pl.ds(h * self.n, self.n)
                    self.z[h].recv()
                    fin(h, rows, self.pb[rows] + self.rb[2, rows].astype(F32) + self.rb[1, rows].astype(F32))

            def sent(self):
                for x in [self.c0, self.c2] + self.z:
                    x.sent()

        def ag_loop(gather, body):
            def step(k, carry):
                gather.arrive(k)
                body(blk_ag(k))
                return carry

            lax.fori_loop(0, 4, step, 0)

        def W(name, lo=0, rows=None):
            first, total = d.w[name]
            return v.wv[pl.ds(first + lo, total if rows is None else rows)]

        def gain(i):
            return gains_ref[pl.ds(i, 1)]

        sx = [Swap(x_ref.at[pl.ds(h * HR, HR)], v.xb.at[pl.ds(h * HR, HR)]) for h in range(PARTS)]
        saux, scot = Swap(aux_ref, v.aux), Swap(cot_ref, v.cotb)
        senc = Swap(e_ref, v.encf.at[z])
        weights = {name: Weight(name) for name in wnames}
        ag1, ag2, ag3 = (Gather(f, R, PARTS) for f in (v.h1f, v.h2f, v.h3f))
        agd3, agd2, agd1 = (Gather(f, R, PARTS) for f in (v.d3f, v.d2f, v.d1f))
        agenc = Gather(v.encf, E, 1)
        rs1, rs2, rs3, rs4, rs5 = (Scatter(v.pb, v.sb, v.rb, R, PARTS) for _ in range(5))
        rso = Scatter(v.opb, v.osb, v.orb, R, 1)
        rse = Scatter(v.epb, v.esb, v.erb, E, 1)
        out_lo, out_eg = Swap(v.lov, lo_ref), Swap(v.egv, eg_ref)
        out_ig = [Swap(v.igv.at[pl.ds(h * HR, HR)], ig_ref.at[pl.ds(h * HR, HR)]) for h in range(PARTS)]

        class Reduce:
            def __init__(self, name):
                self.base, self.rows, self.loc, self.land = d.groups[name]
                self.sl = sl = self.rows // d.nd
                self.tile = 96 if sl % 96 == 0 else sl
                at = lambda f: pl.ds(pl.multiple_of(self.base + f * sl, 16), sl)
                here = pl.ds(self.land, sl)
                self.own = at(dl)
                self.to = [
                    Xfer(v.gsend.at[at(f)], v.grecv.at[k, here], peer)
                    for k, (f, peer) in enumerate(zip(flips[1:], peers[1:]))
                ]
                self.zx = Xfer(v.gsend.at[self.own], v.gz.at[here], z2)
                self.keep = Local(v.gfo.at[here], gout_ref.at[self.own])
                self.spread = [Xfer(v.gfo.at[here], gout_ref.at[self.own], peer) for peer in peers[1:]]
                self.core = [Xfer(v.gfo.at[here], gout_ref.at[self.own], sib)] + [
                    Xfer(gout_ref.at[at(f)], gout_ref.at[at(f)], sib) for f in flips[1:]
                ]

            def tiles(self, rows, body):
                def step(i, carry):
                    body(pl.multiple_of(i * self.tile, 16))
                    return carry

                lax.fori_loop(0, rows // self.tile, step, 0)

            def send(self):
                def cast(r):
                    v.gsend[pl.ds(self.base + r, self.tile)] = v.gf[pl.ds(self.loc + r, self.tile)].astype(BF)

                self.tiles(self.rows, cast)
                for x in self.to:
                    x.start()

            def combine(self):
                for x in self.to:
                    x.recv()

                def add(r):
                    total = v.gf[pl.ds(self.loc + pl.multiple_of(dl * self.sl, 16) + r, self.tile)]
                    for k in range(d.nd - 1):
                        total = total + v.grecv[k, pl.ds(self.land + r, self.tile)].astype(F32)
                    v.gk[pl.ds(self.land + r, self.tile)] = total
                    v.gsend[pl.ds(pl.multiple_of(self.base + dl * self.sl, 16) + r, self.tile)] = total.astype(BF)

                self.tiles(self.sl, add)
                pl.when(is_sw)(self.zx.start)

            def finish(self):
                @pl.when(not_sw)
                def _():
                    self.zx.recv()

                    def add(r):
                        rows = pl.ds(self.land + r, self.tile)
                        v.gfo[rows] = (v.gk[rows] + v.gz[rows].astype(F32)).astype(BF)

                    self.tiles(self.sl, add)
                    self.keep.start()
                    for x in self.spread:
                        x.start()
                    self.core[0].start()

            def relay(self):
                @pl.when(not_sw)
                def _():
                    for x, y in zip(self.spread, self.core[1:]):
                        x.recv()
                        y.start()

            def done(self):
                for x in self.to:
                    x.sent()

                @pl.when(is_sw)
                def _():
                    self.zx.sent()
                    for x in self.core:
                        x.recv()

                @pl.when(not_sw)
                def _():
                    self.keep.wait()
                    for x in self.spread + self.core:
                        x.sent()

        redS, redC, redF = Reduce("S"), Reduce("C"), Reduce("F")

        bar = pltpu.get_barrier_semaphore()
        for dev in [sib, zp, z2] + peers[1:]:
            pl.semaphore_signal(bar, inc=1, device_id={"dp": dev[0], "mp": dev[1]}, device_id_type=MESH)

        @pl.when(is_sw)
        def _():
            pl.semaphore_signal(bar, inc=1, device_id={"dp": mate[0], "mp": mate[1]}, device_id_type=MESH)

        pl.semaphore_wait(bar, 2 + d.nd + sw)

        for x in sx:
            x.start()
        saux.start()
        weights["qkv"].start()

        for h in range(PARTS):
            sx[h].wait()
            rows = pl.ds(h * HR, HR)
            v.h1f[t, rows] = norm_fwd(v.xb[rows].astype(F32), gain(0))
            ag1.send(h)
        weights["so"].start()
        senc.start()
        weights["qkv"].forward()
        saux.wait()

        row16 = lax.broadcasted_iota(jnp.int32, (PADH, R), 0)
        ones_row = jnp.where(row16 == 0, 1.0, 0.0).astype(BF)

        def mask_rows(row, b):
            line = v.aux[pl.ds(row, 1), pl.ds(b * R, R)]
            return jnp.where(row16 == 0, jnp.broadcast_to(line, (PADH, R)), 0.0).astype(BF)

        for b in range(4):
            for h in range(nh):
                v.qa[b, h, pl.ds(hd, PADH)] = ones_row
                v.q2a[b, h, pl.ds(hd, PADH)] = ones_row
                v.ka[b, h, pl.ds(hd, PADH)] = mask_rows(0, b)
        for b in range(d.ne):
            for h in range(nh):
                v.k2a[b, h, pl.ds(hd, PADH)] = mask_rows(1, b)
        for h in range(nh):
            for i in range(2):
                line = v.aux[pl.ds(2 + h, 1), pl.ds(i * 2 * R, 2 * R)]
                v.bias[h, i] = pltpu.roll(jnp.broadcast_to(line, (R, 2 * R)), 0, 1, stride=1, stride_axis=0)[:, :R]
            v.bias[h, 2] = jnp.broadcast_to(v.aux[pl.ds(2 + nh + h, 1), pl.ds(0, R)], (R, R))
        weights["qkv"].wait()

        def project_self(b):
            rows = v.h1f[b]
            q = dot_nt(W("qkv", 0, hc), rows).astype(BF)
            k = dot_nt(W("qkv", hc, hc), rows).astype(BF)
            for h in range(nh):
                v.qa[b, h, pl.ds(0, hd)] = q[h * hd : (h + 1) * hd]
                v.ka[b, h, pl.ds(0, hd)] = k[h * hd : (h + 1) * hd]
            v.vT[b] = dot_nt(W("qkv", 2 * hc, hc), rows).astype(BF)

        ag_loop(ag1, project_self)
        ag1.sent()
        senc.wait()
        agenc.send(0)
        for name in ("cq", "ckv", "co"):
            weights[name].start()
        scot.start()
        weights["so"].forward()

        def attend(b, blocks, qa, ka, vT, out, lse, biased):
            def head(h, carry):
                feat = pl.ds(pl.multiple_of(h * hd, hd), hd)
                q = qa[b, h]

                def block(j, state):
                    m, total, acc = state
                    s = dot_tn(ka[j, h], q)
                    if biased:
                        s = s + v.bias[h, jnp.minimum(b - j, 2)]
                    new = jnp.maximum(m, jnp.max(s, axis=0, keepdims=True))
                    p = jnp.exp(s - new)
                    scale = jnp.exp(m - new)
                    total = total * scale + jnp.sum(p, axis=0, keepdims=True)
                    acc = acc * scale + dot_nn(vT[j, feat], p.astype(BF))
                    return new, total, acc

                first = (jnp.full((1, R), -1e30, F32), jnp.zeros((1, R), F32), jnp.zeros((hd, R), F32))
                m, total, acc = lax.fori_loop(0, blocks, block, first)
                out[b, feat] = (acc / total).astype(BF)
                lse[b, pl.ds(h, 1)] = m + jnp.log(total)
                return carry

            lax.fori_loop(0, nh, head, 0)

        def attend_back(b, blocks, qa, ka, vT, out, lse, dqT, biased):
            def head(h, carry):
                feat = pl.ds(pl.multiple_of(h * hd, hd), hd)
                q, da = qa[b, h], v.da[feat]
                inner = jnp.sum(da.astype(F32) * out[b, feat].astype(F32), axis=0, keepdims=True)
                logsum = lse[b, pl.ds(h, 1)]

                def block(j, dq):
                    k = ka[j, h]
                    s = dot_tn(k, q)
                    if biased:
                        kind = jnp.minimum(b - j, 2)
                        s = s + v.bias[h, kind]
                    p = jnp.exp(s - logsum)
                    ds = p * (dot_tn(vT[j, feat], da) - inner)
                    low = ds.astype(BF)
                    v.dka[j, h] += dot_nt(q, low)
                    v.dva[j, feat] += dot_nt(da, p.astype(BF))
                    if biased:
                        v.dsacc[h, kind] += ds
                    return dq + dot_nn(k, low)

                dq = lax.fori_loop(0, blocks, block, jnp.zeros((ha, R), F32))
                dqT[b, feat] = dq[:hd].astype(BF)
                return carry

            lax.fori_loop(0, nh, head, 0)

        weights["so"].wait()

        def self_out_part(b):
            attend(b, b + 1, v.qa, v.ka, v.vT, v.o1, v.lse1, True)
            v.pb[...] = dot_tn(v.o1[b], W("so"))

        rs1.loop(self_out_part)
        agenc.near()
        agenc.far()
        for name in ("cq", "ckv", "co"):
            weights[name].forward()
        agenc.last()
        agenc.sent()
        weights["ckv"].wait()
        per = R // E
        for b in range(4):
            rows = v.encf[b]
            lanes = pl.ds((b % per) * E, E)
            k = dot_nt(W("ckv", 0, hc), rows).astype(BF)
            for h in range(nh):
                v.k2a[b // per, h, pl.ds(0, hd), lanes] = k[h * hd : (h + 1) * hd]
            v.v2T[b // per, :, lanes] = dot_nt(W("ckv", hc, hc), rows).astype(BF)

        def fin1(h, rows, total):
            x1 = v.xb[rows].astype(F32) + total
            v.x1[rows] = x1
            v.h2f[t, rows] = norm_fwd(x1, gain(1))
            ag2.send(h)

        rs1.finish(fin1)
        rs1.sent()
        for name in ("gu", "fo"):
            weights[name].start()

        weights["cq"].wait()

        def cross_block(b):
            q = dot_nt(W("cq"), v.h2f[b]).astype(BF)
            for h in range(nh):
                v.q2a[b, h, pl.ds(0, hd)] = q[h * hd : (h + 1) * hd]
            attend(b, d.ne, v.q2a, v.k2a, v.v2T, v.o2, v.lse2, False)

        ag_loop(ag2, cross_block)
        ag2.sent()
        scot.wait()
        v.d3f[t] = v.cotb[...]
        for h in range(PARTS):
            agd3.send(h)
        weights["co"].wait()

        def cross_out_part(b):
            v.pb[...] = dot_tn(v.o2[b], W("co"))

        rs2.loop(cross_out_part)
        for name in ("gu", "fo"):
            weights[name].forward()
        agd3.near()
        agd3.far()

        def fin2(h, rows, total):
            x2 = v.x1[rows] + total
            v.x2[rows] = x2
            v.h3f[t, rows] = norm_fwd(x2, gain(2))
            ag3.send(h)

        rs2.finish(fin2)
        rs2.sent()
        agd3.last()
        agd3.sent()
        for name in ("gu", "fo"):
            weights[name].wait()

        fc = 128

        def hidden_block(b):
            def chunk(i, carry):
                r = pl.multiple_of(i * fc, fc)
                rows, back = v.h3f[b], v.d3f[b]
                gu, fo = d.w["gu"][0], d.w["fo"][0]
                gate = dot_nt(v.wv[pl.ds(gu + r, fc)], rows)
                up = dot_nt(v.wv[pl.ds(gu + F + r, fc)], rows)
                sq = gate * gate
                th = jnp.tanh(gate * (GELU_C + (GELU_C * 0.044715) * sq))
                half = 0.5 + 0.5 * th
                gelu = gate * half
                slope = half + gate * (0.5 - 0.5 * th * th) * (GELU_C + (3.0 * GELU_C * 0.044715) * sq)
                v.actT[b, pl.ds(r, fc)] = (gelu * up).astype(BF)
                dact = dot_nt(v.wv[pl.ds(fo + r, fc)], back)
                v.dguT[b, pl.ds(r, fc)] = (dact * up * slope).astype(BF)
                v.dguT[b, pl.ds(F + r, fc)] = (dact * gelu).astype(BF)
                return carry

            lax.fori_loop(0, F // fc, chunk, 0)

        ag_loop(ag3, hidden_block)
        ag3.sent()

        def hidden_back_part(b):
            v.pb[...] = dot_tn(v.dguT[b], W("gu"))

        rs3.loop(hidden_back_part)

        def grads(at, lhs, rows, rhs, tile):
            def step(i, carry):
                r = pl.multiple_of(i * tile, 64)
                total = dot_nn(lhs[0, pl.ds(r, tile)], rhs[0])
                for b in range(1, 4):
                    total = total + dot_nn(lhs[b, pl.ds(r, tile)], rhs[b])
                v.gf[pl.ds(at + r, tile)] = total
                return carry

            lax.fori_loop(0, rows // tile, step, 0)

        def loc(name, group):
            base, _, at, _ = d.groups[group]
            return d.w[name][0] - base + at

        grads(loc("gu", "F"), v.dguT, 2 * F, v.h3f, 256)

        def add_gain(i, h, part):
            if h == 0:
                v.smc[pl.ds(i, 1)] = part
            else:
                v.smc[pl.ds(i, 1)] += part

        v.smc[...] = jnp.zeros(v.smc.shape, F32)

        def fin3(h, rows, total):
            grad, part = norm_bwd(v.x2[rows], gain(2), total)
            add_gain(2, h, part)
            g2 = v.cotb[rows].astype(F32) + grad
            v.gb[rows] = g2
            v.d2f[t, rows] = g2.astype(BF)
            agd2.send(h)

        rs3.finish(fin3)
        rs3.sent()
        grads(loc("fo", "F"), v.actT, F, v.d3f, 256)
        redF.send()

        v.dka[...] = jnp.zeros(v.dka.shape, F32)
        v.dva[...] = jnp.zeros(v.dva.shape, F32)

        def cross_back_block(b):
            v.da[...] = dot_nt(W("co"), v.d2f[b]).astype(BF)
            attend_back(b, d.ne, v.q2a, v.k2a, v.v2T, v.o2, v.lse2, v.dq2T, False)

        ag_loop(agd2, cross_back_block)
        agd2.sent()

        def cross_q_part(b):
            v.pb[...] = dot_tn(v.dq2T[b], W("cq"))

        rs4.loop(cross_q_part)
        for b in range(4):
            lanes = pl.ds((b % per) * E, E)
            for h in range(nh):
                v.dkv2T[b, pl.ds(h * hd, hd)] = v.dka[b // per, h, pl.ds(0, hd), lanes].astype(BF)
            v.dkv2T[b, pl.ds(hc, hc)] = v.dva[b // per, :, lanes].astype(BF)
        redF.combine()
        grads(loc("cq", "C"), v.dq2T, hc, v.h2f, hc)
        grads(loc("co", "C"), v.o2, hc, v.d2f, hc)
        grads(loc("ckv", "C"), v.dkv2T, 2 * hc, v.encf, hc)

        def fin4(h, rows, total):
            grad, part = norm_bwd(v.x1[rows], gain(1), total)
            add_gain(1, h, part)
            g1 = v.gb[rows] + grad
            v.gb[rows] = g1
            v.d1f[t, rows] = g1.astype(BF)
            agd1.send(h)

        rs4.finish(fin4)
        rs4.sent()
        redC.send()

        v.dka[...] = jnp.zeros(v.dka.shape, F32)
        v.dva[...] = jnp.zeros(v.dva.shape, F32)
        v.dsacc[...] = jnp.zeros(v.dsacc.shape, F32)

        def self_back_block(b):
            v.da[...] = dot_nt(W("so"), v.d1f[b]).astype(BF)
            attend_back(b, b + 1, v.qa, v.ka, v.vT, v.o1, v.lse1, v.dqkvT, True)

        ag_loop(agd1, self_back_block)
        agd1.sent()
        redF.finish()
        redC.combine()

        def enc_part(b):
            v.epb[...] = dot_tn(v.dkv2T[b], W("ckv"))

        rse.loop(enc_part)

        for b in range(4):
            for h in range(nh):
                v.dqkvT[b, pl.ds(hc + h * hd, hd)] = v.dka[b, h, pl.ds(0, hd)].astype(BF)
            v.dqkvT[b, pl.ds(2 * hc, hc)] = v.dva[b].astype(BF)
        grads(loc("qkv", "S"), v.dqkvT, 3 * hc, v.h1f, hc)
        grads(loc("so", "S"), v.o1, hc, v.d1f, hc)
        redS.send()

        def self_qkv_part(b):
            v.pb[...] = dot_tn(v.dqkvT[b], W("qkv"))

        rs5.loop(self_qkv_part)

        def hidden_out_part(b):
            v.opb[...] = dot_tn(v.actT[b], W("fo"))

        rso.loop(hidden_out_part)
        redC.finish()
        redF.relay()

        iota0 = lax.broadcasted_iota(jnp.int32, (R, R), 0)
        iota1 = lax.broadcasted_iota(jnp.int32, (R, R), 1)
        flip = (iota0 + iota1 == R - 1).astype(F32)

        def diagonals(h, i):
            turned = lax.dot_general(
                flip, v.dsacc[h, i], (((1,), (0,)), ((), ())), precision=lax.Precision.HIGHEST, preferred_element_type=F32
            )
            wide = jnp.concatenate([turned, jnp.zeros((R, R), F32)], axis=1)
            return jnp.sum(pltpu.roll(wide, 0, 1, stride=1, stride_axis=0), axis=0, keepdims=True)

        lane = lax.broadcasted_iota(jnp.int32, (1, 2 * R), 1)
        for h in range(nh):
            near, off = diagonals(h, 0), diagonals(h, 1)
            far = jnp.sum(jnp.sum(v.dsacc[h, 2], axis=0, keepdims=True), axis=1, keepdims=True)
            off = off + jnp.where(lane == 2 * R - 1, far, 0.0)
            line = jnp.concatenate([pltpu.roll(near, R + 1, 1)[:, :R], off], axis=1)
            for q in range(4):
                v.smc[pl.ds(3 + q * nh + h, 1), pl.ds(0, 3 * R)] = jnp.where(t == q, line, 0.0)

        def fin5(h, rows, total):
            grad, part = norm_bwd(v.xb[rows].astype(F32), gain(0), total)
            add_gain(0, h, part)
            v.igv[rows] = (v.gb[rows] + grad).astype(BF)
            out_ig[h].start()

        rs5.finish(fin5)
        rs5.sent()
        redS.combine()

        def fin_out(h, rows, total):
            v.lov[rows] = (v.x2[rows] + total).astype(BF)

        rso.finish(fin_out)
        rso.sent()
        out_lo.start()

        def fin_enc(h, rows, total):
            v.egv[rows] = total.astype(BF)

        rse.finish(fin_enc)
        rse.sent()
        out_eg.start()

        steps = [sib, zp, z2] + peers[1:3]
        v.sms[0] = v.smc[...]
        small = [Xfer(v.sms.at[i], v.smr.at[i], dev) for i, dev in enumerate(steps)]
        for i, x in enumerate(small):
            x.start()
            if i == 1:
                redC.relay()
            if i == 2:
                redS.finish()
            x.recv()
            v.sms[i + 1] = v.sms[i] + v.smr[i]
        sm_ref[...] = v.sms[len(steps)]
        redS.relay()

        for x in small:
            x.sent()
        for x in [saux, scot, senc] + sx:
            x.sent()
        for name in wnames:
            weights[name].sent()
        for x in [out_lo, out_eg] + out_ig:
            x.wait()
            x.sent()
        for r in (redF, redC, redS):
            r.done()

    return kernel


def local_fn(mesh):
    def local(x_in, enc_in, cotangent, dec_len, enc_len, self_qkv, self_out, cross_q, cross_kv, cross_out, ff_in, ff_out, gains, table):
        d = make_dims(mesh, x_in, enc_in, self_qkv, ff_in, table)
        R, D, hc, nh, F = d.R, d.D, d.hc, d.nh, d.F
        hbm = pl.BlockSpec(memory_space=pl.ANY)
        vmem = pl.BlockSpec(memory_space=pltpu.VMEM)
        ws = {
            "qkv": jnp.transpose(self_qkv, (1, 2, 0)).reshape(3 * hc, D),
            "so": self_out,
            "cq": jnp.transpose(cross_q),
            "ckv": jnp.transpose(cross_kv, (1, 2, 0)).reshape(2 * hc, D),
            "co": cross_out,
            "gu": jnp.transpose(ff_in, (1, 2, 0)).reshape(2 * F, D),
            "fo": ff_out,
        }
        lane = jnp.arange(4 * R, dtype=jnp.int32)
        dist = jnp.where(lane < 2 * R, lane, jnp.where(lane < 3 * R, lane - R, lane - 3 * R))
        onehot = (bucket_index(dist)[:, None] == jnp.arange(NB)[None, :]).astype(BF)
        lines = jnp.einsum("vh,lv->hl", table, onehot, preferred_element_type=F32)
        lines = jnp.where((lane >= R) & (lane < 2 * R), MASK_FILL, lines)
        pos = lane[None, :]
        aux = jnp.concatenate(
            [
                jnp.where(pos < dec_len[0], 0.0, MASK_FILL),
                jnp.where(pos < enc_len[0], 0.0, MASK_FILL),
                lines,
                jnp.broadcast_to(table[NB - 1].astype(F32)[:, None], (nh, 4 * R)),
                jnp.zeros((d.axr - 2 - 2 * nh, 4 * R), F32),
            ],
            axis=0,
        )
        gains_f = gains.astype(F32)
        outs = pl.pallas_call(
            build_kernel(d),
            out_shape=(
                jax.ShapeDtypeStruct((R, D), BF),
                jax.ShapeDtypeStruct((R, D), BF),
                jax.ShapeDtypeStruct((d.E, D), BF),
                jax.ShapeDtypeStruct((d.rows, D), BF),
                jax.ShapeDtypeStruct((d.small, D), F32),
            ),
            in_specs=[hbm, hbm, hbm, hbm, vmem] + [hbm] * len(d.w),
            out_specs=(hbm, hbm, hbm, hbm, vmem),
            scratch_shapes=[pltpu.VMEM(shape, dtype) for _, shape, dtype in scratch_list(d)]
            + [pltpu.SemaphoreType.DMA((SEMS,))] * 3,
            compiler_params=pltpu.CompilerParams(collective_id=0, has_side_effects=True, vmem_limit_bytes=63 << 20),
        )(x_in, enc_in, cotangent, aux, gains_f, *[ws[name] for name in d.w])
        lo, ig, eg, gw, sm = outs
        others = d.ndp // (2 * d.nd)
        if others > 1:
            gw, sm = lax.psum((gw.astype(F32), sm), "dp")
            gw, sm = gw * (1.0 / (2 * d.nd)), sm * (1.0 / (2 * d.nd))
        g = {name: gw[first : first + rows].astype(F32) for name, (first, rows) in d.w.items()}
        mine = lax.dynamic_slice_in_dim(sm, 3 + lax.axis_index("mp") * nh, nh, axis=0)
        col = jnp.arange(D)
        dist = jnp.where(col < R, col, jnp.where(col < 3 * R - 1, col - R + 1, 4 * R))
        pick = (bucket_index(dist)[:, None] == jnp.arange(NB)[None, :]).astype(F32)
        table_grad = jnp.einsum("hl,lv->vh", mine, pick, precision=lax.Precision.HIGHEST, preferred_element_type=F32)
        return (
            lo,
            ig.astype(F32),
            eg.astype(F32),
            jnp.transpose(g["qkv"].reshape(3, hc, D), (2, 0, 1)),
            g["so"],
            jnp.transpose(g["cq"]),
            jnp.transpose(g["ckv"].reshape(2, hc, D), (2, 0, 1)),
            g["co"],
            jnp.transpose(g["gu"].reshape(2, F, D), (2, 0, 1)),
            g["fo"],
            sm[:3],
            table_grad,
        )

    return local


def solution(mesh):
    rows = P(("dp", "mp"), None)
    in_specs = (
        rows, rows, rows, P("dp"), P("dp"), P(None, None, "mp"), P("mp", None), P(None, "mp"), P(None, None, "mp"),
        P("mp", None), P(None, None, "mp"), P("mp", None), P(), P(None, "mp"),
    )
    out_specs = (
        rows, rows, rows, P(None, None, "mp"), P("mp", None), P(None, "mp"), P(None, None, "mp"), P("mp", None),
        P(None, None, "mp"), P("mp", None), P(), P(None, "mp"),
    )
    return jax.shard_map(local_fn(mesh), mesh=mesh, in_specs=in_specs, out_specs=out_specs, check_vma=False)
```

time: 913 us -> 266 us (0.29); the launches traced: 904 us -> 266 us
  waiting for transfers between devices: 583 us -> 0 us
  Pallas kernels: 0 us -> 238 us
  matrix products: 137 us -> 2.72 us
  blocking collectives: 78.6 us -> 0 us
  local copies, waits for them, and re-layouts: 48.2 us -> 11.5 us
  other arithmetic: 39.2 us -> 11.6 us
  between operations: 16.7 us -> 1.98 us
    reduce_scatter x7 -> x0, waiting for transfers between devices: 297 us -> none  [the longest x3 183 us: spread_rows(): lax.psum_scatter(product(jnp.int32(0), rows_here * lax.axis_size('mp')),...]
    pallas_call x0 -> x1, Pallas kernels: none -> 238 us  [local(): pl.pallas_call(build_kernel(d), out_shape=(jax.ShapeDtypeStruct((R, D), B...]
    all_gather x6 -> x0, waiting for transfers between devices: 157 us -> none  [the longest x3 106 us: gather_back(): return lax.all_gather(grad_rows, 'mp', axis=0, tiled=True)]
    dot_general x61 -> x2, matrix products: 137 us -> 2.72 us  [the longest x1 1.72 us: local(): jnp.einsum('hl,lv->vh', mine, pick, precision=lax.Precision.HIGHEST, pref...]
    psum x1 -> x0, waiting for transfers between devices: 127 us -> none  [local(): lax.psum((self_qkv_grad, self_out_grad, cross_q_grad, cross_kv_grad, cros...]
    psum x2 -> x0, blocking collectives: 54.2 us -> none  [the longest x1 40.2 us: local(): lax.psum(jnp.stack([gain_one, gain_two, gain_three]), ('dp', 'mp'))]
    unnamed x228 -> x5, local copies, waits for them, and re-layouts: 28.4 us -> 0.75 us
    all_gather x1 -> x0, blocking collectives: 24.4 us -> none  [local(): enc_full = lax.all_gather(enc_in, 'mp', axis=0, tiled=True)]
  transfers between devices with their start and end apart: 14 -> 0, of which waited for: 12 -> 0; matrix products, arithmetic and copies ran while one was open for 13% -> 0% of each run, Pallas kernels for 0% -> 0%
where the time goes in v1:
time: 266 us
  Pallas kernels  238 us (89%)
  other arithmetic  11.6 us (4%)
  local copies, waits for them, and re-layouts  11.5 us (4%)
  matrix products  2.72 us (1%)
    pallas_call x1, Pallas kernels, local(): pl.pallas_call(build_kernel(d), out_shape=(jax.ShapeDtypeStruct((R, D), B...  238 us

profile of v1, /device:TPU:0, one launch (start us, length us, event | category | flops | bytes accessed | tf_op | source)
XLA Modules:
  0.0 265.8 jit_solution(13546547554511083929)
XLA Ops:
  1.9 0.9 convert_reduce_fusion
  2.8 0.1 pad.3.clone
  2.9 1.0 fusion
  3.9 0.7 maximum_maximum_fusion.refs_3_
  4.6 1.3 convert_element_type.261.refs_4_
  5.9 4.9 %copy.26 = bf16[2,512,768]{2,1,0:T(8,128)(2,1)} copy(bf16[2,512,768]{1,0,2:T(2,128)(2,1)} %bitcast.34) | data formatting | bytes 3145728 | tf_op jit(solution)/shard_map/transpose | solution.py:863
  10.8 238.0 %shard_map.229 = (bf16[256,768]{1,0:T(8,128)(2,1)}, bf16[256,768]{1,0:T(8,128)(2,1)}, bf16[128,768]{1,0:T(8,128)(2,1)}, bf16[3072,768]{1,0:T(8,128)(2,1)}, f32[16,768]{1,0:T(8,128)}) custom-call(bf16[256,768]{1,0:T(8,128)(2,1)} %refs_0_.1, bf16[128,768]{1,0:T(8,128)(2,1)} %refs_1_.1, bf16[256,768]{1,0:T(8,128)(2,1)} %refs_2_.1, ...), custom_call_target="tpu_custom_call" | custom-call | tf_op jit(solution)/shard_map/pallas_call | solution.py:883
  248.9 1.7 fusion.1
  250.6 1.3 slice.35
  251.9 0.0 copy-start
  251.9 1.8 convert_element_type.263
  253.8 1.1 slice.31
  254.9 1.1 convert_bitcast_fusion.1
  256.0 1.9 convert_element_type.262
  257.9 0.0 copy-done
  257.9 0.1 slice.28
  258.0 1.4 convert_bitcast_fusion
  259.3 1.3 slice_convert_fusion
  260.6 0.1 slice.33
  260.7 1.2 slice_convert_fusion.1
  261.9 0.0 copy-start.1
  261.9 3.2 %copy.27 = f32[2,512,768]{1,0,2:T(2,128)} copy(bf16[2,512,768]{2,1,0:T(8,128)(2,1)S(1)} %bitcast.30) | data formatting | bytes 4718592 | tf_op jit(solution)/shard_map/transpose | solution.py:918
  265.1 0.0 copy-done.1
  265.1 0.7 copy.31
  (4 shorter events, 0.1 us)
Async XLA Ops:
  251.9 6.0 %copy-start = (bf16[3072,768]{1,0:T(8,128)(2,1)S(1)}, bf16[3072,768]{1,0:T(8,128)(2,1)}, u32[]{:S(2)}) copy-start(bf16[3072,768]{1,0:T(8,128)(2,1)} %get-tuple-element.20) | copy-start | bytes 14155780
  261.9 3.2 %copy-start.1 = (bf16[256,768]{1,0:T(8,128)(2,1)S(1)}, bf16[256,768]{1,0:T(8,128)(2,1)}, u32[]{:S(2)}) copy-start(bf16[256,768]{1,0:T(8,128)(2,1)} %get-tuple-element.39) | copy-start | bytes 1179652

commit v2 on v1

--- a/solution.py
+++ b/solution.py
@@ -83,11 +83,11 @@
     s, c = 4 * hc, 4 * hc
     d.groups = {}
     land = 0
-    for name, base, rows, loc in (("S", 0, s, 0), ("C", s, c, s), ("F", s + c, 3 * F, 0)):
-        d.groups[name] = (base, rows, loc, land)
+    for name, base, rows in (("S", 0, s), ("C", s, c), ("G", s + c, 2 * F), ("H", s + c + 2 * F, F)):
+        d.groups[name] = (base, rows, 0, land)
         land += rows // d.nd
     d.land = land
-    d.locrows = max(s + c, 3 * F)
+    d.locrows = max(s, c, 2 * F)
     d.small = -(-(3 + 4 * d.nh) // 8) * 8
     return d
 
@@ -95,24 +95,26 @@
 def scratch_list(d):
     R, D, hc, nh, hd, ha, F, E = d.R, d.D, d.hc, d.nh, d.hd, d.ha, d.F, d.E
     full = ((4, R, D), BF)
+    pair = ((2, 2, R, D), BF)
+    HR = R // 2
     return [
         ("xb", (R, D), BF), ("cotb", (R, D), BF), ("aux", (d.axr, 4 * R), F32), ("wv", (d.rows, D), BF),
-        ("h1f",) + full, ("h2f",) + full, ("h3f",) + full, ("d3f",) + full, ("d2f",) + full, ("d1f",) + full,
+        ("h1f",) + full, ("h2f",) + pair, ("h3f",) + pair, ("d3f",) + pair, ("d2f",) + pair, ("d1f",) + full,
         ("encf", (4, E, D), BF),
         ("qa", (4, nh, ha, R), BF), ("ka", (4, nh, ha, R), BF), ("vT", (4, hc, R), BF), ("o1", (4, hc, R), BF),
-        ("q2a", (4, nh, ha, R), BF), ("k2a", (d.ne, nh, ha, R), BF), ("v2T", (d.ne, hc, R), BF), ("o2", (4, hc, R), BF),
-        ("lse1", (4, 8, R), F32), ("lse2", (4, 8, R), F32),
+        ("q2a", (2, 2, nh, ha, R), BF), ("k2a", (d.ne, nh, ha, R), BF), ("v2T", (d.ne, hc, R), BF), ("o2", (2, 2, hc, R), BF),
+        ("lse1", (4, 8, R), F32), ("lse2", (2, 2, 8, R), F32),
         ("bias", (nh, 3, R, R), F32), ("dsacc", (nh, 3, R, R), F32),
         ("x1", (R, D), F32), ("x2", (R, D), F32), ("gb", (R, D), F32),
-        ("pb", (R, D), F32), ("sb", (3, R, D), BF), ("rb", (3, R, D), BF),
-        ("opb", (R, D), F32), ("osb", (3, R, D), BF), ("orb", (3, R, D), BF), ("lov", (R, D), BF), ("igv", (R, D), BF),
-        ("epb", (E, D), F32), ("esb", (3, E, D), BF), ("erb", (3, E, D), BF), ("egv", (E, D), BF),
-        ("actT", (4, F, R), BF), ("dguT", (4, 2 * F, R), BF),
-        ("da", (hc, R), BF), ("dqkvT", (4, 3 * hc, R), BF), ("dq2T", (4, hc, R), BF), ("dkv2T", (4, 2 * hc, E), BF),
+        ("pb", (R, D), F32), ("pf", (R, D), F32), ("sb", (2, 3, HR, D), BF), ("rb", (2, 3, HR, D), BF),
+        ("opb", (R, D), F32), ("osb", (2, 3, HR, D), BF), ("orb", (2, 3, HR, D), BF), ("lov", (R, D), BF), ("igv", (R, D), BF),
+        ("epb", (E, D), F32), ("esb", (1, 3, E, D), BF), ("erb", (1, 3, E, D), BF), ("egv", (E, D), BF),
+        ("actT", (2, 2, F, R), BF), ("dguT", (2, 2, 2 * F, R), BF), ("gus", (3 * F, R), F32),
+        ("da", (hc, R), BF), ("dqkvT", (4, 3 * hc, R), BF), ("dq2T", (2, 2, hc, R), BF), ("dkv2T", (4, 2 * hc, E), BF),
         ("dka", (4, nh, ha, R), F32), ("dva", (4, hc, R), F32),
         ("gf", (d.locrows, D), F32), ("gsend", (d.rows, D), BF), ("grecv", (max(d.nd - 1, 1), d.land, D), BF),
         ("gz", (d.land, D), BF), ("gk", (d.land, D), F32), ("gfo", (d.land, D), BF),
-        ("smc", (d.small, D), F32), ("sms", (6, d.small, D), F32), ("smr", (5, d.small, D), F32),
+        ("smc", (d.small, D), F32), ("sms", (3, d.small, D), F32), ("smr", (7, d.small, D), F32),
     ]
 
 
@@ -142,6 +144,7 @@
         sib = (dp + 1 - 2 * c, z)
         zp = (dp, z + 1 - 2 * a)
         z2 = (dp, z + 2 - 4 * u)
+        z3 = (dp, 3 - z)
         mate = (2 * chip + u, a + 2 * c)
         d0, d1 = dl % 2, dl // 2
         flips = [dl, dl + 1 - 2 * d0, dl + 2 - 4 * d1, 3 - dl][: d.nd]
@@ -156,8 +159,8 @@
             return count[0] - 1
 
         class Xfer:
-            def __init__(self, src, dst, dev):
-                self.i, self.src, self.dst, self.dev = new_id(), src, dst, dev
+            def __init__(self, src, dst, dev, i=None):
+                self.i, self.src, self.dst, self.dev = new_id() if i is None else i, src, dst, dev
 
             def desc(self):
                 return pltpu.make_async_remote_copy(
@@ -203,12 +206,15 @@
                 pl.when(is_sw)(self.far.sent)
 
         class Weight:
-            def __init__(self, name):
+            def __init__(self, name, piece=0, pieces=1):
                 first, rows = d.w[name]
+                rows = rows // pieces
+                at = piece * rows
+                first += at
                 sl = rows // d.nd
-                mine = pl.ds(pl.multiple_of(dl * sl, 16), sl)
+                mine = pl.ds(pl.multiple_of(at + dl * sl, 16), sl)
                 here = v.wv.at[pl.ds(pl.multiple_of(first + dl * sl, 16), sl)]
-                self.near = Local(w_refs[name], v.wv.at[pl.ds(first, rows)])
+                self.near = Local(w_refs[name].at[pl.ds(at, rows)], v.wv.at[pl.ds(first, rows)])
                 self.far = Xfer(w_refs[name].at[mine], here, mate)
                 self.on = [Xfer(here, here, peer) for peer in peers[1:]]
 
@@ -281,32 +287,82 @@
                 for x in self.z + self.c + self.f:
                     x.sent()
 
+        class PairGather:
+            def __init__(self, full):
+                self.full, self.ids = full, [new_id() for _ in range(6)][0]
+
+            def own(self, h):
+                return self.full.at[h, a, pl.ds(pl.multiple_of(c * HR, HR), HR)]
+
+            def z(self, h):
+                return Xfer(self.own(h), self.own(h), zp, self.ids + h)
+
+            def c(self, h):
+                return Xfer(self.own(h), self.own(h), sib, self.ids + 2 + h)
+
+            def f(self, h):
+                there = self.full.at[h, 1 - a, pl.ds(pl.multiple_of(c * HR, HR), HR)]
+                return Xfer(there, there, sib, self.ids + 4 + h)
+
+            def send(self, h):
+                self.z(h).start()
+                self.c(h).start()
+
+            def near(self, h):
+                self.c(h).recv()
+
+            def pass_on(self, h):
+                self.z(h).recv()
+                self.f(h).start()
+
+            def last(self, h):
+                self.f(h).recv()
+
+            def sent(self):
+                for h in range(2):
+                    for x in (self.z(h), self.c(h), self.f(h)):
+                        x.sent()
+
         class Scatter:
-            def __init__(self, pb, sb, rb, rows, parts):
-                self.pb, self.sb, self.rb, self.parts, self.n = pb, sb, rb, parts, rows // parts
-                at = lambda r, i, h: r.at[i, pl.ds(h * self.n, self.n)]
-                self.c0 = Xfer(sb.at[0], rb.at[0], sib)
-                self.z = [Xfer(at(sb, 1, h), at(rb, 1, h), zp) for h in range(parts)]
-                self.c2 = Xfer(sb.at[2], rb.at[2], sib)
+            def __init__(self, pb, sb, rb):
+                self.pb, self.sb, self.rb = pb, sb, rb
+                self.parts, self.n = sb.shape[0], sb.shape[2]
+                self.ids = [new_id() for _ in range(3 * self.parts)][0]
+
+            def rows(self, h):
+                return pl.ds(h * self.n if isinstance(h, int) else pl.multiple_of(h * self.n, self.n), self.n)
+
+            def x(self, slot, h, dev):
+                return Xfer(self.sb.at[h, slot], self.rb.at[h, slot], dev, self.ids + slot * self.parts + h)
+
+            def c0(self, h):
+                return self.x(0, h, sib)
+
+            def z(self, h):
+                return self.x(1, h, zp)
+
+            def c2(self, h):
+                return self.x(2, h, sib)
 
             def emit(self, k):
                 @pl.when(k == 0)
                 def _():
-                    self.sb[0] = self.pb[...].astype(BF)
-                    self.c0.start()
+                    for h in range(self.parts):
+                        self.sb[h, 0] = self.pb[self.rows(h)].astype(BF)
+                        self.c0(h).start()
 
                 @pl.when(k == 1)
                 def _():
-                    self.c0.recv()
                     for h in range(self.parts):
-                        rows = pl.ds(h * self.n, self.n)
-                        self.sb[1, rows] = (self.pb[rows] + self.rb[0, rows].astype(F32)).astype(BF)
-                        self.z[h].start()
+                        self.c0(h).recv()
+                        self.sb[h, 1] = (self.pb[self.rows(h)] + self.rb[h, 0].astype(F32)).astype(BF)
+                        self.z(h).start()
 
                 @pl.when(k == 2)
                 def _():
-                    self.sb[2] = self.pb[...].astype(BF)
-                    self.c2.start()
+                    for h in range(self.parts):
+                        self.sb[h, 2] = self.pb[self.rows(h)].astype(BF)
+                        self.c2(h).start()
 
             def loop(self, partial):
                 def step(k, carry):
@@ -316,16 +372,36 @@
 
                 lax.fori_loop(0, 4, step, 0)
 
-            def finish(self, fin):
-                self.c2.recv()
+            def emit_pair(self, h, partial, kick=True):
+                mine = pl.ds(pl.multiple_of(c * HR, HR), HR)
+                other = pl.ds(pl.multiple_of((1 - c) * HR, HR), HR)
+                v.pf[...] = partial(h, 1 - a)
+                self.sb[h, 0] = v.pf[other].astype(BF)
+                self.c0(h).start()
+                self.sb[h, 1] = v.pf[mine].astype(BF)
+                v.pf[...] = partial(h, a)
+                self.sb[h, 2] = v.pf[other].astype(BF)
+                self.c2(h).start()
+                self.pb[self.rows(h)] = v.pf[mine]
+                self.c0(h).recv()
+                self.sb[h, 1] = (self.sb[h, 1].astype(F32) + self.rb[h, 0].astype(F32)).astype(BF)
+                if kick:
+                    self.z(h).start()
+
+            def kick(self):
                 for h in range(self.parts):
-                    rows = pl.ds(h * self.n, self.n)
-                    self.z[h].recv()
-                    fin(h, rows, self.pb[rows] + self.rb[2, rows].astype(F32) + self.rb[1, rows].astype(F32))
+                    self.z(h).start()
+
+            def finish(self, h, fin):
+                self.c2(h).recv()
+                self.z(h).recv()
+                rows = self.rows(h)
+                fin(h, rows, self.pb[rows] + self.rb[h, 2].astype(F32) + self.rb[h, 1].astype(F32))
 
             def sent(self):
-                for x in [self.c0, self.c2] + self.z:
-                    x.sent()
+                for h in range(self.parts):
+                    for x in (self.c0(h), self.z(h), self.c2(h)):
+                        x.sent()
 
         def ag_loop(gather, body):
             def step(k, carry):
@@ -335,6 +411,27 @@
 
             lax.fori_loop(0, 4, step, 0)
 
+        def halves(gather, body, scatter, partial, after=None):
+            def half(h, carry):
+                def step(k, inner):
+                    pl.when(k == 0)(lambda: gather.near(h))
+
+                    @pl.when(k == 1)
+                    def _():
+                        gather.pass_on(h)
+                        gather.last(h)
+
+                    body(h, a + k - 2 * a * k)
+                    return inner
+
+                lax.fori_loop(0, 2, step, 0)
+                scatter.emit_pair(h, partial)
+                if after is not None:
+                    after(h)
+                return carry
+
+            lax.fori_loop(0, 2, half, 0)
+
         def W(name, lo=0, rows=None):
             first, total = d.w[name]
             return v.wv[pl.ds(first + lo, total if rows is None else rows)]
@@ -345,13 +442,14 @@
         sx = [Swap(x_ref.at[pl.ds(h * HR, HR)], v.xb.at[pl.ds(h * HR, HR)]) for h in range(PARTS)]
         saux, scot = Swap(aux_ref, v.aux), Swap(cot_ref, v.cotb)
         senc = Swap(e_ref, v.encf.at[z])
-        weights = {name: Weight(name) for name in wnames}
-        ag1, ag2, ag3 = (Gather(f, R, PARTS) for f in (v.h1f, v.h2f, v.h3f))
-        agd3, agd2, agd1 = (Gather(f, R, PARTS) for f in (v.d3f, v.d2f, v.d1f))
+        weights = {name: Weight(name) for name in wnames if name != "qkv"}
+        qkv3 = [Weight("qkv", i, 3) for i in range(3)]
+        ag1, agd1 = (Gather(f, R, PARTS) for f in (v.h1f, v.d1f))
+        ag2, ag3, agd3, agd2 = (PairGather(f) for f in (v.h2f, v.h3f, v.d3f, v.d2f))
         agenc = Gather(v.encf, E, 1)
-        rs1, rs2, rs3, rs4, rs5 = (Scatter(v.pb, v.sb, v.rb, R, PARTS) for _ in range(5))
-        rso = Scatter(v.opb, v.osb, v.orb, R, 1)
-        rse = Scatter(v.epb, v.esb, v.erb, E, 1)
+        rs1, rs2, rs3, rs4, rs5 = (Scatter(v.pb, v.sb, v.rb) for _ in range(5))
+        rso = Scatter(v.opb, v.osb, v.orb)
+        rse = Scatter(v.epb, v.esb, v.erb)
         out_lo, out_eg = Swap(v.lov, lo_ref), Swap(v.egv, eg_ref)
         out_ig = [Swap(v.igv.at[pl.ds(h * HR, HR)], ig_ref.at[pl.ds(h * HR, HR)]) for h in range(PARTS)]
 
@@ -389,12 +487,19 @@
                 for x in self.to:
                     x.start()
 
+                def keep(r):
+                    v.gk[pl.ds(self.land + r, self.tile)] = v.gf[
+                        pl.ds(self.loc + pl.multiple_of(dl * self.sl, 16) + r, self.tile)
+                    ]
+
+                self.tiles(self.sl, keep)
+
             def combine(self):
                 for x in self.to:
                     x.recv()
 
                 def add(r):
-                    total = v.gf[pl.ds(self.loc + pl.multiple_of(dl * self.sl, 16) + r, self.tile)]
+                    total = v.gk[pl.ds(self.land + r, self.tile)]
                     for k in range(d.nd - 1):
                         total = total + v.grecv[k, pl.ds(self.land + r, self.tile)].astype(F32)
                     v.gk[pl.ds(self.land + r, self.tile)] = total
@@ -441,22 +546,23 @@
                     for x in self.spread + self.core:
                         x.sent()
 
-        redS, redC, redF = Reduce("S"), Reduce("C"), Reduce("F")
+        redS, redC, redG, redH = (Reduce(name) for name in "SCGH")
 
         bar = pltpu.get_barrier_semaphore()
-        for dev in [sib, zp, z2] + peers[1:]:
+        for dev in [sib, zp, z2, z3] + peers[1:]:
             pl.semaphore_signal(bar, inc=1, device_id={"dp": dev[0], "mp": dev[1]}, device_id_type=MESH)
 
         @pl.when(is_sw)
         def _():
             pl.semaphore_signal(bar, inc=1, device_id={"dp": mate[0], "mp": mate[1]}, device_id_type=MESH)
 
-        pl.semaphore_wait(bar, 2 + d.nd + sw)
+        pl.semaphore_wait(bar, 3 + d.nd + sw)
 
         for x in sx:
             x.start()
         saux.start()
-        weights["qkv"].start()
+        for x in qkv3:
+            x.start()
 
         for h in range(PARTS):
             sx[h].wait()
@@ -465,7 +571,10 @@
             ag1.send(h)
         weights["so"].start()
         senc.start()
-        weights["qkv"].forward()
+        for name in ("ckv", "cq", "co"):
+            weights[name].start()
+        for x in qkv3:
+            x.forward()
         saux.wait()
 
         row16 = lax.broadcasted_iota(jnp.int32, (PADH, R), 0)
@@ -478,7 +587,7 @@
         for b in range(4):
             for h in range(nh):
                 v.qa[b, h, pl.ds(hd, PADH)] = ones_row
-                v.q2a[b, h, pl.ds(hd, PADH)] = ones_row
+                v.q2a[b // 2, b % 2, h, pl.ds(hd, PADH)] = ones_row
                 v.ka[b, h, pl.ds(hd, PADH)] = mask_rows(0, b)
         for b in range(d.ne):
             for h in range(nh):
@@ -488,187 +597,223 @@
                 line = v.aux[pl.ds(2 + h, 1), pl.ds(i * 2 * R, 2 * R)]
                 v.bias[h, i] = pltpu.roll(jnp.broadcast_to(line, (R, 2 * R)), 0, 1, stride=1, stride_axis=0)[:, :R]
             v.bias[h, 2] = jnp.broadcast_to(v.aux[pl.ds(2 + nh + h, 1), pl.ds(0, R)], (R, R))
-        weights["qkv"].wait()
+
+        @pl.when(is_sw)
+        def _():
+            ag1.near()
+            ag1.far()
+
+        for x in qkv3:
+            x.wait()
 
         def project_self(b):
-            rows = v.h1f[b]
-            q = dot_nt(W("qkv", 0, hc), rows).astype(BF)
-            k = dot_nt(W("qkv", hc, hc), rows).astype(BF)
+            qkv = dot_nt(W("qkv"), v.h1f[b]).astype(BF)
             for h in range(nh):
-                v.qa[b, h, pl.ds(0, hd)] = q[h * hd : (h + 1) * hd]
-                v.ka[b, h, pl.ds(0, hd)] = k[h * hd : (h + 1) * hd]
-            v.vT[b] = dot_nt(W("qkv", 2 * hc, hc), rows).astype(BF)
-
-        ag_loop(ag1, project_self)
-        ag1.sent()
+                v.qa[b, h, pl.ds(0, hd)] = qkv[h * hd : (h + 1) * hd]
+                v.ka[b, h, pl.ds(0, hd)] = qkv[hc + h * hd : hc + (h + 1) * hd]
+            v.vT[b] = qkv[2 * hc :]
+
+        def project_step(k, carry):
+            pl.when((k == 1) & not_sw)(ag1.near)
+            pl.when((k == 2) & not_sw)(ag1.far)
+            pl.when(k == 3)(ag1.last)
+            pl.when(k == 2)(weights["so"].forward)
+            project_self(blk_ag(k))
+            return carry
+
+        lax.fori_loop(0, 4, project_step, 0)
         senc.wait()
         agenc.send(0)
-        for name in ("cq", "ckv", "co"):
-            weights[name].start()
-        scot.start()
-        weights["so"].forward()
-
-        def attend(b, blocks, qa, ka, vT, out, lse, biased):
-            def head(h, carry):
-                feat = pl.ds(pl.multiple_of(h * hd, hd), hd)
-                q = qa[b, h]
-
-                def block(j, state):
-                    m, total, acc = state
-                    s = dot_tn(ka[j, h], q)
-                    if biased:
-                        s = s + v.bias[h, jnp.minimum(b - j, 2)]
+
+        def feat(h):
+            return pl.ds(h * hd, hd)
+
+        def attend_self(b):
+            qs = [v.qa[b, h] for h in range(nh)]
+
+            def block(j, state):
+                out = []
+                for h in range(nh):
+                    m, total, acc = state[h]
+                    s = dot_tn(v.ka[j, h], qs[h]) + v.bias[h, jnp.minimum(b - j, 2)]
                     new = jnp.maximum(m, jnp.max(s, axis=0, keepdims=True))
                     p = jnp.exp(s - new)
                     scale = jnp.exp(m - new)
                     total = total * scale + jnp.sum(p, axis=0, keepdims=True)
-                    acc = acc * scale + dot_nn(vT[j, feat], p.astype(BF))
-                    return new, total, acc
-
-                first = (jnp.full((1, R), -1e30, F32), jnp.zeros((1, R), F32), jnp.zeros((hd, R), F32))
-                m, total, acc = lax.fori_loop(0, blocks, block, first)
-                out[b, feat] = (acc / total).astype(BF)
-                lse[b, pl.ds(h, 1)] = m + jnp.log(total)
-                return carry
-
-            lax.fori_loop(0, nh, head, 0)
-
-        def attend_back(b, blocks, qa, ka, vT, out, lse, dqT, biased):
-            def head(h, carry):
-                feat = pl.ds(pl.multiple_of(h * hd, hd), hd)
-                q, da = qa[b, h], v.da[feat]
-                inner = jnp.sum(da.astype(F32) * out[b, feat].astype(F32), axis=0, keepdims=True)
-                logsum = lse[b, pl.ds(h, 1)]
-
-                def block(j, dq):
-                    k = ka[j, h]
-                    s = dot_tn(k, q)
-                    if biased:
-                        kind = jnp.minimum(b - j, 2)
-                        s = s + v.bias[h, kind]
-                    p = jnp.exp(s - logsum)
-                    ds = p * (dot_tn(vT[j, feat], da) - inner)
-                    low = ds.astype(BF)
+                    out.append((new, total, acc * scale + dot_nn(v.vT[j, feat(h)], p.astype(BF))))
+                return tuple(out)
+
+            first = (jnp.full((1, R), -1e30, F32), jnp.zeros((1, R), F32), jnp.zeros((hd, R), F32))
+            state = lax.fori_loop(0, b + 1, block, (first,) * nh)
+            for h in range(nh):
+                m, total, acc = state[h]
+                v.o1[b, feat(h)] = (acc / total).astype(BF)
+                v.lse1[b, pl.ds(h, 1)] = m + jnp.log(total)
+
+        def attend_cross(i, j):
+            for h in range(nh):
+                q = v.q2a[i, j, h]
+                s = [dot_tn(v.k2a[e, h], q) for e in range(d.ne)]
+                m = jnp.max(s[0], axis=0, keepdims=True)
+                for part in s[1:]:
+                    m = jnp.maximum(m, jnp.max(part, axis=0, keepdims=True))
+                p = [jnp.exp(part - m) for part in s]
+                total = sum(jnp.sum(part, axis=0, keepdims=True) for part in p)
+                acc = sum(dot_nn(v.v2T[e, feat(h)], part.astype(BF)) for e, part in enumerate(p))
+                v.o2[i, j, feat(h)] = (acc / total).astype(BF)
+                v.lse2[i, j, pl.ds(h, 1)] = m + jnp.log(total)
+
+        def tile_back(h, q, k, vals, da, inner, logsum, bias):
+            s = dot_tn(k, q)
+            if bias is not None:
+                s = s + bias
+            p = jnp.exp(s - logsum)
+            ds = p * (dot_tn(vals, da) - inner)
+            return p.astype(BF), ds, ds.astype(BF)
+
+        def head_back(h, q, out, lse):
+            da = v.da[feat(h)]
+            inner = jnp.sum(da.astype(F32) * out.astype(F32), axis=0, keepdims=True)
+            return q, da, inner, lse
+
+        def attend_self_back(b):
+            heads = [head_back(h, v.qa[b, h], v.o1[b, feat(h)], v.lse1[b, pl.ds(h, 1)]) for h in range(nh)]
+
+            def block(j, dqs):
+                kind = jnp.minimum(b - j, 2)
+                out = []
+                for h in range(nh):
+                    q, da, inner, logsum = heads[h]
+                    k = v.ka[j, h]
+                    p, ds, low = tile_back(h, q, k, v.vT[j, feat(h)], da, inner, logsum, v.bias[h, kind])
                     v.dka[j, h] += dot_nt(q, low)
-                    v.dva[j, feat] += dot_nt(da, p.astype(BF))
-                    if biased:
-                        v.dsacc[h, kind] += ds
-                    return dq + dot_nn(k, low)
-
-                dq = lax.fori_loop(0, blocks, block, jnp.zeros((ha, R), F32))
-                dqT[b, feat] = dq[:hd].astype(BF)
-                return carry
-
-            lax.fori_loop(0, nh, head, 0)
-
-        weights["so"].wait()
-
-        def self_out_part(b):
-            attend(b, b + 1, v.qa, v.ka, v.vT, v.o1, v.lse1, True)
+                    v.dva[j, feat(h)] += dot_nt(da, p)
+                    v.dsacc[h, kind] += ds
+                    out.append(dqs[h] + dot_nn(k, low))
+                return tuple(out)
+
+            dqs = lax.fori_loop(0, b + 1, block, (jnp.zeros((ha, R), F32),) * nh)
+            for h in range(nh):
+                v.dqkvT[b, feat(h)] = dqs[h][:hd].astype(BF)
+
+        def attend_cross_back(i, j):
+            for h in range(nh):
+                q, da, inner, logsum = head_back(h, v.q2a[i, j, h], v.o2[i, j, feat(h)], v.lse2[i, j, pl.ds(h, 1)])
+                dq = jnp.zeros((ha, R), F32)
+                for e in range(d.ne):
+                    k = v.k2a[e, h]
+                    p, ds, low = tile_back(h, q, k, v.v2T[e, feat(h)], da, inner, logsum, None)
+                    v.dka[e, h] += dot_nt(q, low)
+                    v.dva[e, feat(h)] += dot_nt(da, p)
+                    dq = dq + dot_nn(k, low)
+                v.dq2T[i, j, feat(h)] = dq[:hd].astype(BF)
+
+        def self_forward(k, carry):
+            b = blk_rs(k)
+            attend_self(b)
+            pl.when(k == 0)(weights["so"].wait)
             v.pb[...] = dot_tn(v.o1[b], W("so"))
-
-        rs1.loop(self_out_part)
-        agenc.near()
-        agenc.far()
-        for name in ("cq", "ckv", "co"):
-            weights[name].forward()
+            rs1.emit(k)
+            pl.when(k == 1)(scot.start)
+            pl.when(k == 1)(agenc.near)
+            pl.when(k == 1)(agenc.far)
+            for name in ("ckv", "cq", "co"):
+                pl.when(k == 2)(weights[name].forward)
+            return carry
+
+        lax.fori_loop(0, 4, self_forward, 0)
         agenc.last()
-        agenc.sent()
         weights["ckv"].wait()
         per = R // E
         for b in range(4):
-            rows = v.encf[b]
             lanes = pl.ds((b % per) * E, E)
-            k = dot_nt(W("ckv", 0, hc), rows).astype(BF)
+            kv = dot_nt(W("ckv"), v.encf[b]).astype(BF)
             for h in range(nh):
-                v.k2a[b // per, h, pl.ds(0, hd), lanes] = k[h * hd : (h + 1) * hd]
-            v.v2T[b // per, :, lanes] = dot_nt(W("ckv", hc, hc), rows).astype(BF)
+                v.k2a[b // per, h, pl.ds(0, hd), lanes] = kv[h * hd : (h + 1) * hd]
+            v.v2T[b // per, :, lanes] = kv[hc:]
 
         def fin1(h, rows, total):
             x1 = v.xb[rows].astype(F32) + total
             v.x1[rows] = x1
-            v.h2f[t, rows] = norm_fwd(x1, gain(1))
+            v.h2f[h, a, pl.ds(pl.multiple_of(c * HR, HR), HR)] = norm_fwd(x1, gain(1))
             ag2.send(h)
 
-        rs1.finish(fin1)
-        rs1.sent()
+        for h in range(2):
+            rs1.finish(h, fin1)
         for name in ("gu", "fo"):
             weights[name].start()
 
         weights["cq"].wait()
-
-        def cross_block(b):
-            q = dot_nt(W("cq"), v.h2f[b]).astype(BF)
+        weights["co"].wait()
+
+        def cross_block(i, j):
+            q = dot_nt(W("cq"), v.h2f[i, j]).astype(BF)
             for h in range(nh):
-                v.q2a[b, h, pl.ds(0, hd)] = q[h * hd : (h + 1) * hd]
-            attend(b, d.ne, v.q2a, v.k2a, v.v2T, v.o2, v.lse2, False)
-
-        ag_loop(ag2, cross_block)
-        ag2.sent()
-        scot.wait()
-        v.d3f[t] = v.cotb[...]
-        for h in range(PARTS):
+                v.q2a[i, j, h, pl.ds(0, hd)] = q[h * hd : (h + 1) * hd]
+            attend_cross(i, j)
+
+        def send_cot(h):
+            pl.when(h == 0)(scot.wait)
+            rows = pl.ds(pl.multiple_of(h * HR, HR), HR)
+            v.d3f[h, a, pl.ds(pl.multiple_of(c * HR, HR), HR)] = v.cotb[rows]
             agd3.send(h)
-        weights["co"].wait()
-
-        def cross_out_part(b):
-            v.pb[...] = dot_tn(v.o2[b], W("co"))
-
-        rs2.loop(cross_out_part)
+
+        rs1.sent()
+        halves(ag2, cross_block, rs2, lambda i, j: dot_tn(v.o2[i, j], W("co")), send_cot)
         for name in ("gu", "fo"):
             weights[name].forward()
-        agd3.near()
-        agd3.far()
 
         def fin2(h, rows, total):
             x2 = v.x1[rows] + total
             v.x2[rows] = x2
-            v.h3f[t, rows] = norm_fwd(x2, gain(2))
+            v.h3f[h, a, pl.ds(pl.multiple_of(c * HR, HR), HR)] = norm_fwd(x2, gain(2))
             ag3.send(h)
 
-        rs2.finish(fin2)
-        rs2.sent()
-        agd3.last()
-        agd3.sent()
+        for h in range(2):
+            rs2.finish(h, fin2)
+        for h in range(2):
+            agd3.near(h)
+            agd3.pass_on(h)
+        for h in range(2):
+            agd3.last(h)
         for name in ("gu", "fo"):
             weights[name].wait()
 
-        fc = 128
-
-        def hidden_block(b):
-            def chunk(i, carry):
-                r = pl.multiple_of(i * fc, fc)
-                rows, back = v.h3f[b], v.d3f[b]
-                gu, fo = d.w["gu"][0], d.w["fo"][0]
-                gate = dot_nt(v.wv[pl.ds(gu + r, fc)], rows)
-                up = dot_nt(v.wv[pl.ds(gu + F + r, fc)], rows)
+        fc = 64
+
+        def hidden_block(i, j):
+            rows = v.h3f[i, j]
+            v.gus[pl.ds(0, F)] = dot_nt(W("gu", 0, F), rows)
+            v.gus[pl.ds(F, F)] = dot_nt(W("gu", F, F), rows)
+            v.gus[pl.ds(2 * F, F)] = dot_nt(W("fo"), v.d3f[i, j])
+
+            def chunk(n, carry):
+                r = pl.multiple_of(n * fc, fc)
+                gate, up, dact = (v.gus[pl.ds(m * F + r, fc)] for m in range(3))
                 sq = gate * gate
                 th = jnp.tanh(gate * (GELU_C + (GELU_C * 0.044715) * sq))
                 half = 0.5 + 0.5 * th
                 gelu = gate * half
                 slope = half + gate * (0.5 - 0.5 * th * th) * (GELU_C + (3.0 * GELU_C * 0.044715) * sq)
-                v.actT[b, pl.ds(r, fc)] = (gelu * up).astype(BF)
-                dact = dot_nt(v.wv[pl.ds(fo + r, fc)], back)
-                v.dguT[b, pl.ds(r, fc)] = (dact * up * slope).astype(BF)
-                v.dguT[b, pl.ds(F + r, fc)] = (dact * gelu).astype(BF)
+                v.actT[i, j, pl.ds(r, fc)] = (gelu * up).astype(BF)
+                v.dguT[i, j, pl.ds(r, fc)] = (dact * up * slope).astype(BF)
+                v.dguT[i, j, pl.ds(F + r, fc)] = (dact * gelu).astype(BF)
                 return carry
 
             lax.fori_loop(0, F // fc, chunk, 0)
 
-        ag_loop(ag3, hidden_block)
-        ag3.sent()
-
-        def hidden_back_part(b):
-            v.pb[...] = dot_tn(v.dguT[b], W("gu"))
-
-        rs3.loop(hidden_back_part)
+        rs2.sent()
+        halves(ag3, hidden_block, rs3, lambda i, j: dot_tn(v.dguT[i, j], W("gu")))
 
         def grads(at, lhs, rows, rhs, tile):
+            spots = [(b,) for b in range(4)] if len(lhs.shape) == 3 else [(b // 2, b % 2) for b in range(4)]
+
             def step(i, carry):
                 r = pl.multiple_of(i * tile, 64)
-                total = dot_nn(lhs[0, pl.ds(r, tile)], rhs[0])
-                for b in range(1, 4):
-                    total = total + dot_nn(lhs[b, pl.ds(r, tile)], rhs[b])
+                total = None
+                for spot in spots:
+                    part = dot_nn(lhs[spot + (pl.ds(r, tile),)], rhs[spot])
+                    total = part if total is None else total + part
                 v.gf[pl.ds(at + r, tile)] = total
                 return carry
 
@@ -677,8 +822,6 @@
         def loc(name, group):
             base, _, at, _ = d.groups[group]
             return d.w[name][0] - base + at
-
-        grads(loc("gu", "F"), v.dguT, 2 * F, v.h3f, 256)
 
         def add_gain(i, h, part):
             if h == 0:
@@ -693,37 +836,25 @@
             add_gain(2, h, part)
             g2 = v.cotb[rows].astype(F32) + grad
             v.gb[rows] = g2
-            v.d2f[t, rows] = g2.astype(BF)
+            v.d2f[h, a, pl.ds(pl.multiple_of(c * HR, HR), HR)] = g2.astype(BF)
             agd2.send(h)
 
-        rs3.finish(fin3)
-        rs3.sent()
-        grads(loc("fo", "F"), v.actT, F, v.d3f, 256)
-        redF.send()
+        rs3.finish(0, fin3)
+        grads(loc("gu", "G"), v.dguT, 2 * F, v.h3f, 256)
+        redG.send()
+        rs3.finish(1, fin3)
+        grads(loc("fo", "H"), v.actT, F, v.d3f, 256)
+        redH.send()
 
         v.dka[...] = jnp.zeros(v.dka.shape, F32)
         v.dva[...] = jnp.zeros(v.dva.shape, F32)
 
-        def cross_back_block(b):
-            v.da[...] = dot_nt(W("co"), v.d2f[b]).astype(BF)
-            attend_back(b, d.ne, v.q2a, v.k2a, v.v2T, v.o2, v.lse2, v.dq2T, False)
-
-        ag_loop(agd2, cross_back_block)
-        agd2.sent()
-
-        def cross_q_part(b):
-            v.pb[...] = dot_tn(v.dq2T[b], W("cq"))
-
-        rs4.loop(cross_q_part)
-        for b in range(4):
-            lanes = pl.ds((b % per) * E, E)
-            for h in range(nh):
-                v.dkv2T[b, pl.ds(h * hd, hd)] = v.dka[b // per, h, pl.ds(0, hd), lanes].astype(BF)
-            v.dkv2T[b, pl.ds(hc, hc)] = v.dva[b // per, :, lanes].astype(BF)
-        redF.combine()
-        grads(loc("cq", "C"), v.dq2T, hc, v.h2f, hc)
-        grads(loc("co", "C"), v.o2, hc, v.d2f, hc)
-        grads(loc("ckv", "C"), v.dkv2T, 2 * hc, v.encf, hc)
+        def cross_back_block(i, j):
+            v.da[...] = dot_nt(W("co"), v.d2f[i, j]).astype(BF)
+            attend_cross_back(i, j)
+
+        rs3.sent()
+        halves(agd2, cross_back_block, rs4, lambda i, j: dot_tn(v.dq2T[i, j], W("cq")))
 
         def fin4(h, rows, total):
             grad, part = norm_bwd(v.x1[rows], gain(1), total)
@@ -733,27 +864,40 @@
             v.d1f[t, rows] = g1.astype(BF)
             agd1.send(h)
 
-        rs4.finish(fin4)
-        rs4.sent()
+        rs4.finish(0, fin4)
+        for b in range(4):
+            lanes = pl.ds((b % per) * E, E)
+            for h in range(nh):
+                v.dkv2T[b, pl.ds(h * hd, hd)] = v.dka[b // per, h, pl.ds(0, hd), lanes].astype(BF)
+            v.dkv2T[b, pl.ds(hc, hc)] = v.dva[b // per, :, lanes].astype(BF)
+        rs4.finish(1, fin4)
+        redG.combine()
+        grads(loc("cq", "C"), v.dq2T, hc, v.h2f, hc)
+        grads(loc("co", "C"), v.o2, hc, v.d2f, hc)
+        grads(loc("ckv", "C"), v.dkv2T, 2 * hc, v.encf, hc)
         redC.send()
+
+        def hidden_out(h, carry):
+            rso.emit_pair(h, lambda i, j: dot_tn(v.actT[i, j], W("fo")), kick=False)
+            return carry
+
+        lax.fori_loop(0, 2, hidden_out, 0)
 
         v.dka[...] = jnp.zeros(v.dka.shape, F32)
         v.dva[...] = jnp.zeros(v.dva.shape, F32)
         v.dsacc[...] = jnp.zeros(v.dsacc.shape, F32)
 
-        def self_back_block(b):
+        def self_back(k, carry):
+            b = blk_ag(k)
+            agd1.arrive(k)
+            pl.when(k == 1)(rso.kick)
+            pl.when(k == 2)(redH.combine)
+            pl.when(k == 3)(redG.finish)
             v.da[...] = dot_nt(W("so"), v.d1f[b]).astype(BF)
-            attend_back(b, b + 1, v.qa, v.ka, v.vT, v.o1, v.lse1, v.dqkvT, True)
-
-        ag_loop(agd1, self_back_block)
-        agd1.sent()
-        redF.finish()
-        redC.combine()
-
-        def enc_part(b):
-            v.epb[...] = dot_tn(v.dkv2T[b], W("ckv"))
-
-        rse.loop(enc_part)
+            attend_self_back(b)
+            return carry
+
+        lax.fori_loop(0, 4, self_back, 0)
 
         for b in range(4):
             for h in range(nh):
@@ -766,14 +910,22 @@
         def self_qkv_part(b):
             v.pb[...] = dot_tn(v.dqkvT[b], W("qkv"))
 
+        redC.combine()
+        rs4.sent()
         rs5.loop(self_qkv_part)
-
-        def hidden_out_part(b):
-            v.opb[...] = dot_tn(v.actT[b], W("fo"))
-
-        rso.loop(hidden_out_part)
-        redC.finish()
-        redF.relay()
+        redH.finish()
+
+        def fin_out(h, rows, total):
+            v.lov[rows] = (v.x2[rows] + total).astype(BF)
+
+        for h in range(2):
+            rso.finish(h, fin_out)
+        out_lo.start()
+
+        def enc_part(b):
+            v.epb[...] = dot_tn(v.dkv2T[b], W("ckv"))
+
+        rse.loop(enc_part)
 
         iota0 = lax.broadcasted_iota(jnp.int32, (R, R), 0)
         iota1 = lax.broadcasted_iota(jnp.int32, (R, R), 1)
@@ -799,50 +951,62 @@
             grad, part = norm_bwd(v.xb[rows].astype(F32), gain(0), total)
             add_gain(0, h, part)
             v.igv[rows] = (v.gb[rows] + grad).astype(BF)
-            out_ig[h].start()
-
-        rs5.finish(fin5)
-        rs5.sent()
+
+        for h in range(2):
+            rs5.finish(h, fin5)
+
+        plane = peers[1:]
+        lines = [zp, z2, z3]
+        v.sms[0] = v.smc[...]
+        first = [Xfer(v.sms.at[0], v.smr.at[i], dev) for i, dev in enumerate(lines)]
+        second = [Xfer(v.sms.at[1], v.smr.at[3 + i], dev) for i, dev in enumerate(plane)]
+        third = [Xfer(v.sms.at[2], v.smr.at[6], sib)]
+        for x in first:
+            x.start()
+        out_ig[0].start()
+        redC.finish()
         redS.combine()
-
-        def fin_out(h, rows, total):
-            v.lov[rows] = (v.x2[rows] + total).astype(BF)
-
-        rso.finish(fin_out)
-        rso.sent()
-        out_lo.start()
+        out_ig[1].start()
+        for x in first:
+            x.recv()
+        v.sms[1] = (v.sms[0] + v.smr[0]) + (v.smr[1] + v.smr[2])
+        for x in second:
+            x.start()
 
         def fin_enc(h, rows, total):
             v.egv[rows] = total.astype(BF)
 
-        rse.finish(fin_enc)
-        rse.sent()
+        rse.finish(0, fin_enc)
         out_eg.start()
-
-        steps = [sib, zp, z2] + peers[1:3]
-        v.sms[0] = v.smc[...]
-        small = [Xfer(v.sms.at[i], v.smr.at[i], dev) for i, dev in enumerate(steps)]
-        for i, x in enumerate(small):
-            x.start()
-            if i == 1:
-                redC.relay()
-            if i == 2:
-                redS.finish()
+        for x in second:
             x.recv()
-            v.sms[i + 1] = v.sms[i] + v.smr[i]
-        sm_ref[...] = v.sms[len(steps)]
+        if len(plane) == 3:
+            v.sms[2] = (v.sms[1] + v.smr[3]) + (v.smr[4] + v.smr[5])
+        elif len(plane) == 1:
+            v.sms[2] = v.sms[1] + v.smr[3]
+        else:
+            v.sms[2] = v.sms[1]
+        third[0].start()
+        redS.finish()
+        third[0].recv()
+        sm_ref[...] = v.sms[2] + v.smr[6]
+        redG.relay()
+        redH.relay()
+        redC.relay()
         redS.relay()
 
-        for x in small:
+        for x in first + second + third:
+            x.sent()
+        for x in (ag1, ag2, ag3, agd1, agd2, agd3, agenc, rs5, rso, rse):
             x.sent()
         for x in [saux, scot, senc] + sx:
             x.sent()
-        for name in wnames:
-            weights[name].sent()
+        for x in list(weights.values()) + qkv3:
+            x.sent()
         for x in [out_lo, out_eg] + out_ig:
             x.wait()
             x.sent()
-        for r in (redF, redC, redS):
+        for r in (redG, redH, redC, redS):
             r.done()
 
     return kernel

time: 266 us -> 237 us (0.89)
  Pallas kernels: 238 us -> 208 us
    pallas_call x1, Pallas kernels: 238 us -> 208 us  [local(): pl.pallas_call(build_kernel(d), out_shape=(jax.ShapeDtypeStruct((R, D), B...]
where the time goes in v2:
time: 237 us; the launch traced here: 236 us
  Pallas kernels  208 us (88%)
  other arithmetic  11.6 us (5%)
  local copies, waits for them, and re-layouts  11.5 us (5%)
  matrix products  2.72 us (1%)
    pallas_call x1, Pallas kernels, local(): pl.pallas_call(build_kernel(d), out_shape=(jax.ShapeDtypeStruct((R, D), B...  208 us
    transpose x1, local copies, waits for them, and re-layouts, local(): jnp.transpose(ff_in, (1, 2, 0)).reshape(2 * F, D)  4.87 us

profile of v2, /device:TPU:0, one launch (start us, length us, event | category | flops | bytes accessed | tf_op | source)
XLA Modules:
  0.0 236.1 jit_solution(4865440811445312624)
XLA Ops:
  1.9 0.9 convert_reduce_fusion
  2.8 0.1 pad.3.clone
  2.9 1.0 fusion
  3.9 0.7 maximum_maximum_fusion.refs_3_
  4.6 1.3 convert_element_type.261.refs_4_
  5.9 4.9 %copy.26 = bf16[2,512,768]{2,1,0:T(8,128)(2,1)} copy(bf16[2,512,768]{1,0,2:T(2,128)(2,1)} %bitcast.34) | data formatting | bytes 3145728 | tf_op jit(solution)/shard_map/transpose | solution.py:1027
  10.8 208.3 %shard_map.229 = (bf16[256,768]{1,0:T(8,128)(2,1)}, bf16[256,768]{1,0:T(8,128)(2,1)}, bf16[128,768]{1,0:T(8,128)(2,1)}, bf16[3072,768]{1,0:T(8,128)(2,1)}, f32[16,768]{1,0:T(8,128)}) custom-call(bf16[256,768]{1,0:T(8,128)(2,1)} %refs_0_.1, bf16[128,768]{1,0:T(8,128)(2,1)} %refs_1_.1, bf16[256,768]{1,0:T(8,128)(2,1)} %refs_2_.1, ...), custom_call_target="tpu_custom_call" | custom-call | tf_op jit(solution)/shard_map/pallas_call | solution.py:1047
  219.1 1.7 fusion.1
  220.9 1.3 slice.35
  222.2 0.0 copy-start
  222.2 1.8 convert_element_type.263
  224.1 1.1 slice.31
  225.2 1.1 convert_bitcast_fusion.1
  226.3 1.9 convert_element_type.262
  228.2 0.0 copy-done
  228.2 0.1 slice.28
  228.2 1.4 convert_bitcast_fusion
  229.6 1.3 slice_convert_fusion
  230.8 0.1 slice.33
  231.0 1.2 slice_convert_fusion.1
  232.2 0.0 copy-start.1
  232.2 3.2 %copy.27 = f32[2,512,768]{1,0,2:T(2,128)} copy(bf16[2,512,768]{2,1,0:T(8,128)(2,1)S(1)} %bitcast.30) | data formatting | bytes 4718592 | tf_op jit(solution)/shard_map/transpose | solution.py:1082
  235.4 0.0 copy-done.1
  235.4 0.7 copy.31
  (4 shorter events, 0.1 us)
Async XLA Ops:
  222.2 6.0 %copy-start = (bf16[3072,768]{1,0:T(8,128)(2,1)S(1)}, bf16[3072,768]{1,0:T(8,128)(2,1)}, u32[]{:S(2)}) copy-start(bf16[3072,768]{1,0:T(8,128)(2,1)} %get-tuple-element.20) | copy-start | bytes 14155780
  232.2 3.2 %copy-start.1 = (bf16[256,768]{1,0:T(8,128)(2,1)S(1)}, bf16[256,768]{1,0:T(8,128)(2,1)}, u32[]{:S(2)}) copy-start(bf16[256,768]{1,0:T(8,128)(2,1)} %get-tuple-element.39) | copy-start | bytes 1179652

commit v3 on v2

--- a/solution.py
+++ b/solution.py
@@ -17,7 +17,7 @@
 PARTS = 2
 PADH = 16
 GELU_C = math.sqrt(2.0 / math.pi)
-SEMS = 224
+SEMS = 256
 
 
 def bucket_index(distance):
@@ -74,16 +74,16 @@
     d.ne = 4 * d.E // d.R
     d.axr = -(-(2 + 2 * d.nh) // 8) * 8
     hc, F = d.hc, d.F
-    names = (("qkv", 3 * hc), ("so", hc), ("cq", hc), ("ckv", 2 * hc), ("co", hc), ("gu", 2 * F), ("fo", F))
+    names = (("gu", 2 * F), ("fo", F), ("qkv", 3 * hc), ("so", hc), ("ckv", 2 * hc), ("cq", hc), ("co", hc))
     d.w, at = {}, 0
     for name, rows in names:
         d.w[name] = (at, rows)
         at += rows
     d.rows = at
-    s, c = 4 * hc, 4 * hc
+    s, c = 3 * hc, 4 * hc
     d.groups = {}
     land = 0
-    for name, base, rows in (("S", 0, s), ("C", s, c), ("G", s + c, 2 * F), ("H", s + c + 2 * F, F)):
+    for name, base, rows in (("G", 0, 2 * F), ("H", 2 * F, F), ("S", 3 * F, s), ("O", 3 * F + s, hc), ("C", 3 * F + s + hc, c)):
         d.groups[name] = (base, rows, 0, land)
         land += rows // d.nd
     d.land = land
@@ -98,7 +98,7 @@
     pair = ((2, 2, R, D), BF)
     HR = R // 2
     return [
-        ("xb", (R, D), BF), ("cotb", (R, D), BF), ("aux", (d.axr, 4 * R), F32), ("wv", (d.rows, D), BF),
+        ("xb", (R, D), BF), ("cotb", (R, D), BF), ("aux", (d.axr, 4 * R), F32), ("aux0", (d.axr, 4 * R), F32), ("ffb", (2, 1024, 128), BF), ("ffs", (1024, 128), F32), ("wv", (d.rows, D), BF),
         ("h1f",) + full, ("h2f",) + pair, ("h3f",) + pair, ("d3f",) + pair, ("d2f",) + pair, ("d1f",) + full,
         ("encf", (4, E, D), BF),
         ("qa", (4, nh, ha, R), BF), ("ka", (4, nh, ha, R), BF), ("vT", (4, hc, R), BF), ("o1", (4, hc, R), BF),
@@ -114,7 +114,7 @@
         ("dka", (4, nh, ha, R), F32), ("dva", (4, hc, R), F32),
         ("gf", (d.locrows, D), F32), ("gsend", (d.rows, D), BF), ("grecv", (max(d.nd - 1, 1), d.land, D), BF),
         ("gz", (d.land, D), BF), ("gk", (d.land, D), F32), ("gfo", (d.land, D), BF),
-        ("smc", (d.small, D), F32), ("sms", (3, d.small, D), F32), ("smr", (7, d.small, D), F32),
+        ("smc", (d.small, D), F32), ("sms", (4, d.small, D), F32), ("smr", (7, d.small, D), F32),
     ]
 
 
@@ -125,14 +125,16 @@
     HR = R // PARTS
 
     def kernel(*refs):
-        x_ref, e_ref, cot_ref, aux_ref, gains_ref = refs[:5]
-        w_refs = dict(zip(wnames, refs[5 : 5 + len(wnames)]))
-        lo_ref, ig_ref, eg_ref, gout_ref, sm_ref = refs[5 + len(wnames) : 10 + len(wnames)]
-        tail = refs[10 + len(wnames) :]
+        x_ref, e_ref, cot_ref, tab_ref, dlen_ref, elen_ref, gains_ref = refs[:7]
+        w_refs = dict(zip(wnames, refs[7 : 7 + len(wnames)]))
+        lo_ref, ig_ref, eg_ref, gout_ref, sm_ref = refs[7 + len(wnames) : 12 + len(wnames)]
+        tail = refs[12 + len(wnames) :]
         v = Dims()
         for name, ref in zip(names, tail):
             setattr(v, name, ref)
         ss, rs, ls = tail[len(names) :]
+        ff_ref = w_refs["gu"]
+        w_refs["gu"] = v.gsend.at[pl.ds(0, 2 * F)]
 
         dp, z = lax.axis_index("dp"), lax.axis_index("mp")
         c, chip = dp % 2, dp // 2
@@ -144,7 +146,6 @@
         sib = (dp + 1 - 2 * c, z)
         zp = (dp, z + 1 - 2 * a)
         z2 = (dp, z + 2 - 4 * u)
-        z3 = (dp, 3 - z)
         mate = (2 * chip + u, a + 2 * c)
         d0, d1 = dl % 2, dl // 2
         flips = [dl, dl + 1 - 2 * d0, dl + 2 - 4 * d1, 3 - dl][: d.nd]
@@ -237,10 +238,11 @@
                     for x in self.on:
                         x.recv()
 
-            def sent(self):
+            def sent(self, first=True):
                 @pl.when(is_sw)
                 def _():
-                    self.far.sent()
+                    if first:
+                        self.far.sent()
                     for x in self.on:
                         x.sent()
 
@@ -344,7 +346,7 @@
             def c2(self, h):
                 return self.x(2, h, sib)
 
-            def emit(self, k):
+            def emit(self, k, kick=True):
                 @pl.when(k == 0)
                 def _():
                     for h in range(self.parts):
@@ -356,7 +358,8 @@
                     for h in range(self.parts):
                         self.c0(h).recv()
                         self.sb[h, 1] = (self.pb[self.rows(h)] + self.rb[h, 0].astype(F32)).astype(BF)
-                        self.z(h).start()
+                        if kick:
+                            self.z(h).start()
 
                 @pl.when(k == 2)
                 def _():
@@ -364,10 +367,10 @@
                         self.sb[h, 2] = self.pb[self.rows(h)].astype(BF)
                         self.c2(h).start()
 
-            def loop(self, partial):
+            def loop(self, partial, kick=True):
                 def step(k, carry):
                     partial(blk_rs(k))
-                    self.emit(k)
+                    self.emit(k, kick)
                     return carry
 
                 lax.fori_loop(0, 4, step, 0)
@@ -437,10 +440,10 @@
             return v.wv[pl.ds(first + lo, total if rows is None else rows)]
 
         def gain(i):
-            return gains_ref[pl.ds(i, 1)]
+            return gains_ref[pl.ds(i, 1)].astype(F32)
 
         sx = [Swap(x_ref.at[pl.ds(h * HR, HR)], v.xb.at[pl.ds(h * HR, HR)]) for h in range(PARTS)]
-        saux, scot = Swap(aux_ref, v.aux), Swap(cot_ref, v.cotb)
+        saux, scot = Swap(v.aux0, v.aux), Swap(cot_ref, v.cotb)
         senc = Swap(e_ref, v.encf.at[z])
         weights = {name: Weight(name) for name in wnames if name != "qkv"}
         qkv3 = [Weight("qkv", i, 3) for i in range(3)]
@@ -546,29 +549,59 @@
                     for x in self.spread + self.core:
                         x.sent()
 
-        redS, redC, redG, redH = (Reduce(name) for name in "SCGH")
+        redS, redO, redC, redG, redH = (Reduce(name) for name in "SOCGH")
 
         bar = pltpu.get_barrier_semaphore()
-        for dev in [sib, zp, z2, z3] + peers[1:]:
+        for dev in [sib, zp, z2] + peers[1:]:
             pl.semaphore_signal(bar, inc=1, device_id={"dp": dev[0], "mp": dev[1]}, device_id_type=MESH)
 
         @pl.when(is_sw)
         def _():
             pl.semaphore_signal(bar, inc=1, device_id={"dp": mate[0], "mp": mate[1]}, device_id_type=MESH)
 
-        pl.semaphore_wait(bar, 3 + d.nd + sw)
+        pl.semaphore_wait(bar, 2 + d.nd + sw)
 
         for x in sx:
             x.start()
-        saux.start()
         for x in qkv3:
             x.start()
-
-        for h in range(PARTS):
-            sx[h].wait()
-            rows = pl.ds(h * HR, HR)
-            v.h1f[t, rows] = norm_fwd(v.xb[rows].astype(F32), gain(0))
-            ag1.send(h)
+        turns = D // 128
+        loads = [Local(ff_ref.at[pl.ds(i * 1024, 1024)], v.ffb.at[i % 2]) for i in range(turns)]
+        loads[0].start()
+
+        def first_norm():
+            for h in range(PARTS):
+                sx[h].wait()
+                rows = pl.ds(h * HR, HR)
+                v.h1f[t, rows] = norm_fwd(v.xb[rows].astype(F32), gain(0))
+                ag1.send(h)
+
+        pl.when(not_sw)(first_norm)
+
+        pos = lax.broadcasted_iota(jnp.int32, (1, 4 * R), 1)
+        dist = jnp.where(pos < 2 * R, pos, jnp.where(pos < 3 * R, pos - R, pos - 3 * R))
+        onehot = jnp.where(lax.broadcasted_iota(jnp.int32, (NB, 4 * R), 0) == bucket_index(dist), 1.0, 0.0).astype(BF)
+        lines = dot_nn(tab_ref[...], onehot)
+        v.aux0[...] = jnp.zeros(v.aux0.shape, F32)
+        v.aux0[pl.ds(0, 1)] = jnp.where(pos < dlen_ref[0], 0.0, MASK_FILL)
+        v.aux0[pl.ds(1, 1)] = jnp.where(pos < elen_ref[0], 0.0, MASK_FILL)
+        v.aux0[pl.ds(2, nh)] = jnp.where((pos >= R) & (pos < 2 * R), MASK_FILL, lines)
+        v.aux0[pl.ds(2 + nh, nh)] = jnp.broadcast_to(lines[:, 2 * R : 2 * R + 1], (nh, 4 * R))
+        saux.start()
+
+        def turn(i):
+            loads[i].wait()
+            if i + 1 < turns:
+                loads[i + 1].start()
+            v.ffs[...] = v.ffb[i % 2].astype(F32)
+            for j in range(8):
+                part = v.ffs[pl.ds(j, 128, stride=8)]
+                v.gsend[pl.ds((j % 2) * F + (j // 2) * 128, 128), pl.ds(i * 128, 128)] = jnp.transpose(part).astype(BF)
+
+        for i in range(turns):
+            turn(i)
+
+        pl.when(is_sw)(first_norm)
         weights["so"].start()
         senc.start()
         for name in ("ckv", "cq", "co"):
@@ -841,10 +874,18 @@
 
         rs3.finish(0, fin3)
         grads(loc("gu", "G"), v.dguT, 2 * F, v.h3f, 256)
+        pl.when(is_sw)(weights["gu"].far.sent)
         redG.send()
+
+        def hidden_out(h, carry):
+            rso.emit_pair(h, lambda i, j: dot_tn(v.actT[i, j], W("fo")), kick=False)
+            return carry
+
+        lax.fori_loop(0, 2, hidden_out, 0)
         rs3.finish(1, fin3)
         grads(loc("fo", "H"), v.actT, F, v.d3f, 256)
         redH.send()
+        rso.kick()
 
         v.dka[...] = jnp.zeros(v.dka.shape, F32)
         v.dva[...] = jnp.zeros(v.dva.shape, F32)
@@ -864,24 +905,29 @@
             v.d1f[t, rows] = g1.astype(BF)
             agd1.send(h)
 
-        rs4.finish(0, fin4)
         for b in range(4):
             lanes = pl.ds((b % per) * E, E)
             for h in range(nh):
                 v.dkv2T[b, pl.ds(h * hd, hd)] = v.dka[b // per, h, pl.ds(0, hd), lanes].astype(BF)
             v.dkv2T[b, pl.ds(hc, hc)] = v.dva[b // per, :, lanes].astype(BF)
-        rs4.finish(1, fin4)
-        redG.combine()
+
+        def enc_part(b):
+            v.epb[...] = dot_tn(v.dkv2T[b], W("ckv"))
+
+        rse.loop(enc_part, kick=False)
         grads(loc("cq", "C"), v.dq2T, hc, v.h2f, hc)
         grads(loc("co", "C"), v.o2, hc, v.d2f, hc)
         grads(loc("ckv", "C"), v.dkv2T, 2 * hc, v.encf, hc)
         redC.send()
-
-        def hidden_out(h, carry):
-            rso.emit_pair(h, lambda i, j: dot_tn(v.actT[i, j], W("fo")), kick=False)
-            return carry
-
-        lax.fori_loop(0, 2, hidden_out, 0)
+        rs4.finish(0, fin4)
+
+        def fin_out(h, rows, total):
+            v.lov[rows] = (v.x2[rows] + total).astype(BF)
+
+        for h in range(2):
+            rso.finish(h, fin_out)
+        rs4.finish(1, fin4)
+        redG.combine()
 
         v.dka[...] = jnp.zeros(v.dka.shape, F32)
         v.dva[...] = jnp.zeros(v.dva.shape, F32)
@@ -890,9 +936,15 @@
         def self_back(k, carry):
             b = blk_ag(k)
             agd1.arrive(k)
-            pl.when(k == 1)(rso.kick)
+            pl.when(k == 2)(out_lo.start)
+            pl.when(k == 3)(rse.kick)
             pl.when(k == 2)(redH.combine)
-            pl.when(k == 3)(redG.finish)
+
+            @pl.when(k == 3)
+            def _():
+                grads(loc("so", "O"), v.o1, hc, v.d1f, hc)
+                redO.send()
+
             v.da[...] = dot_nt(W("so"), v.d1f[b]).astype(BF)
             attend_self_back(b)
             return carry
@@ -904,28 +956,21 @@
                 v.dqkvT[b, pl.ds(hc + h * hd, hd)] = v.dka[b, h, pl.ds(0, hd)].astype(BF)
             v.dqkvT[b, pl.ds(2 * hc, hc)] = v.dva[b].astype(BF)
         grads(loc("qkv", "S"), v.dqkvT, 3 * hc, v.h1f, hc)
-        grads(loc("so", "S"), v.o1, hc, v.d1f, hc)
         redS.send()
 
         def self_qkv_part(b):
             v.pb[...] = dot_tn(v.dqkvT[b], W("qkv"))
 
-        redC.combine()
         rs4.sent()
         rs5.loop(self_qkv_part)
+        redC.combine()
+        redO.combine()
+        redG.finish()
         redH.finish()
 
-        def fin_out(h, rows, total):
-            v.lov[rows] = (v.x2[rows] + total).astype(BF)
-
-        for h in range(2):
-            rso.finish(h, fin_out)
-        out_lo.start()
-
-        def enc_part(b):
-            v.epb[...] = dot_tn(v.dkv2T[b], W("ckv"))
-
-        rse.loop(enc_part)
+        def fin_enc(h, rows, total):
+            v.egv[rows] = total.astype(BF)
+
 
         iota0 = lax.broadcasted_iota(jnp.int32, (R, R), 0)
         iota1 = lax.broadcasted_iota(jnp.int32, (R, R), 1)
@@ -952,48 +997,46 @@
             add_gain(0, h, part)
             v.igv[rows] = (v.gb[rows] + grad).astype(BF)
 
+        plane = peers[1:]
+        lines = [zp, z2]
+        first = [Xfer(v.sms.at[i], v.smr.at[i], dev) for i, dev in enumerate(lines)]
+        second = [Xfer(v.sms.at[2], v.smr.at[3 + i], dev) for i, dev in enumerate(plane)]
+        third = [Xfer(v.sms.at[3], v.smr.at[6], sib)]
+        redS.combine()
         for h in range(2):
             rs5.finish(h, fin5)
-
-        plane = peers[1:]
-        lines = [zp, z2, z3]
         v.sms[0] = v.smc[...]
-        first = [Xfer(v.sms.at[0], v.smr.at[i], dev) for i, dev in enumerate(lines)]
-        second = [Xfer(v.sms.at[1], v.smr.at[3 + i], dev) for i, dev in enumerate(plane)]
-        third = [Xfer(v.sms.at[2], v.smr.at[6], sib)]
-        for x in first:
+        first[0].start()
+        first[0].recv()
+        v.sms[1] = v.sms[0] + v.smr[0]
+        first[1].start()
+        for x in out_ig:
             x.start()
-        out_ig[0].start()
+        redS.finish()
         redC.finish()
-        redS.combine()
-        out_ig[1].start()
-        for x in first:
-            x.recv()
-        v.sms[1] = (v.sms[0] + v.smr[0]) + (v.smr[1] + v.smr[2])
+        redO.finish()
+        first[1].recv()
+        v.sms[2] = v.sms[1] + v.smr[1]
         for x in second:
             x.start()
-
-        def fin_enc(h, rows, total):
-            v.egv[rows] = total.astype(BF)
-
         rse.finish(0, fin_enc)
         out_eg.start()
+        redG.relay()
+        redH.relay()
+        redC.relay()
         for x in second:
             x.recv()
         if len(plane) == 3:
-            v.sms[2] = (v.sms[1] + v.smr[3]) + (v.smr[4] + v.smr[5])
+            v.sms[3] = (v.sms[2] + v.smr[3]) + (v.smr[4] + v.smr[5])
         elif len(plane) == 1:
-            v.sms[2] = v.sms[1] + v.smr[3]
+            v.sms[3] = v.sms[2] + v.smr[3]
         else:
-            v.sms[2] = v.sms[1]
+            v.sms[3] = v.sms[2]
         third[0].start()
-        redS.finish()
+        redO.relay()
+        redS.relay()
         third[0].recv()
-        sm_ref[...] = v.sms[2] + v.smr[6]
-        redG.relay()
-        redH.relay()
-        redC.relay()
-        redS.relay()
+        sm_ref[...] = v.sms[3] + v.smr[6]
 
         for x in first + second + third:
             x.sent()
@@ -1001,15 +1044,81 @@
             x.sent()
         for x in [saux, scot, senc] + sx:
             x.sent()
-        for x in list(weights.values()) + qkv3:
+        for name, x in weights.items():
+            x.sent(name != "gu")
+        for x in qkv3:
             x.sent()
         for x in [out_lo, out_eg] + out_ig:
             x.wait()
             x.sent()
-        for r in (redG, redH, redC, redS):
+        for r in (redG, redH, redC, redO, redS):
             r.done()
 
     return kernel
+
+
+def unpack(d, gw, lo, ig, eg, sm):
+    R, D, F, hc, nh, E = d.R, d.D, d.F, d.hc, d.nh, d.E
+    steps = 3
+    cols = D // steps
+
+    def kernel(gu_ref, fo_ref, qkv_ref, so_ref, ckv_ref, cq_ref, co_ref, lo_ref, ig_ref, eg_ref, sm_ref, *outs):
+        lo_out, ig_out, eg_out, gu_out, fo_out, qkv_out, so_out, ckv_out, cq_out, co_out, gains_out, table_out = outs
+        for j in range(2 * F // 128):
+            part = jnp.transpose(gu_ref[pl.ds((j % 2) * F + (j // 2) * 128, 128)].astype(F32))
+            gu_out[pl.ds(j, cols, stride=2 * F // 128)] = part
+        for src, dst in (
+            (fo_ref, fo_out), (qkv_ref, qkv_out), (so_ref, so_out), (ckv_ref, ckv_out), (cq_ref, cq_out), (co_ref, co_out)
+        ):
+            dst[...] = src[...].astype(F32)
+
+        @pl.when(pl.program_id(0) == 0)
+        def _():
+            lo_out[...] = lo_ref[...]
+            ig_out[...] = ig_ref[...].astype(F32)
+            eg_out[...] = eg_ref[...].astype(F32)
+            gains_out[...] = sm_ref[pl.ds(0, 3)]
+            col = lax.broadcasted_iota(jnp.int32, (1, D), 1)
+            dist = jnp.where(col < R, col, jnp.where(col < 3 * R - 1, col - R + 1, 4 * R))
+            pick = (lax.broadcasted_iota(jnp.int32, (NB, D), 0) == bucket_index(dist)).astype(F32)
+            z = lax.axis_index("mp")
+            mine = jnp.zeros((nh, D), F32)
+            for q in range(4):
+                mine = jnp.where(z == q, sm_ref[pl.ds(3 + q * nh, nh)], mine)
+            table_out[...] = lax.dot_general(
+                mine, pick, (((1,), (1,)), ((), ())), precision=lax.Precision.HIGHEST, preferred_element_type=F32
+            )
+
+    at = lambda name: d.w[name][0]
+    rows = lambda name, n: pl.BlockSpec((n, D), lambda i: (at(name) // n + i, 0))
+    out_rows = lambda n: pl.BlockSpec((n, D), lambda i: (i, 0))
+    whole = lambda *shape: pl.BlockSpec(shape, lambda i: (0,) * len(shape))
+    third = {name: d.w[name][1] // steps for name in ("qkv", "so", "ckv", "cq", "co")}
+    half = F // 2
+    assert all(at(name) % n == 0 for name, n in third.items()) and at("fo") % half == 0 and at("gu") == 0
+    shape = lambda *dims: jax.ShapeDtypeStruct(dims, F32)
+    return pl.pallas_call(
+        kernel,
+        grid=(steps,),
+        in_specs=[
+            pl.BlockSpec((2 * F, cols), lambda i: (0, i)),
+            pl.BlockSpec((half, D), lambda i: (at("fo") // half + jnp.minimum(i, 1), 0)),
+        ]
+        + [rows(name, n) for name, n in third.items()]
+        + [whole(R, D), whole(R, D), whole(E, D), whole(d.small, D)],
+        out_specs=[
+            whole(R, D), whole(R, D), whole(E, D),
+            pl.BlockSpec((cols * 2 * F // 128, 128), lambda i: (i, 0)),
+            pl.BlockSpec((half, D), lambda i: (jnp.minimum(i, 1), 0)),
+        ]
+        + [out_rows(n) for n in third.values()]
+        + [whole(3, D), whole(nh, NB)],
+        out_shape=[
+            jax.ShapeDtypeStruct((R, D), BF), shape(R, D), shape(E, D), shape(D * 2 * F // 128, 128), shape(F, D),
+            shape(3 * hc, D), shape(hc, D), shape(2 * hc, D), shape(hc, D), shape(hc, D), shape(3, D), shape(nh, NB),
+        ],
+        compiler_params=pltpu.CompilerParams(vmem_limit_bytes=63 << 20),
+    )(*[gw] * 7, lo, ig, eg, sm)
 
 
 def local_fn(mesh):
@@ -1018,32 +1127,16 @@
         R, D, hc, nh, F = d.R, d.D, d.hc, d.nh, d.F
         hbm = pl.BlockSpec(memory_space=pl.ANY)
         vmem = pl.BlockSpec(memory_space=pltpu.VMEM)
+        smem = pl.BlockSpec(memory_space=pltpu.SMEM)
         ws = {
             "qkv": jnp.transpose(self_qkv, (1, 2, 0)).reshape(3 * hc, D),
             "so": self_out,
             "cq": jnp.transpose(cross_q),
             "ckv": jnp.transpose(cross_kv, (1, 2, 0)).reshape(2 * hc, D),
             "co": cross_out,
-            "gu": jnp.transpose(ff_in, (1, 2, 0)).reshape(2 * F, D),
+            "gu": jnp.transpose(ff_in.reshape(D, 2, F // 128, 128), (0, 2, 1, 3)).reshape(D * 2 * F // 128, 128),
             "fo": ff_out,
         }
-        lane = jnp.arange(4 * R, dtype=jnp.int32)
-        dist = jnp.where(lane < 2 * R, lane, jnp.where(lane < 3 * R, lane - R, lane - 3 * R))
-        onehot = (bucket_index(dist)[:, None] == jnp.arange(NB)[None, :]).astype(BF)
-        lines = jnp.einsum("vh,lv->hl", table, onehot, preferred_element_type=F32)
-        lines = jnp.where((lane >= R) & (lane < 2 * R), MASK_FILL, lines)
-        pos = lane[None, :]
-        aux = jnp.concatenate(
-            [
-                jnp.where(pos < dec_len[0], 0.0, MASK_FILL),
-                jnp.where(pos < enc_len[0], 0.0, MASK_FILL),
-                lines,
-                jnp.broadcast_to(table[NB - 1].astype(F32)[:, None], (nh, 4 * R)),
-                jnp.zeros((d.axr - 2 - 2 * nh, 4 * R), F32),
-            ],
-            axis=0,
-        )
-        gains_f = gains.astype(F32)
         outs = pl.pallas_call(
             build_kernel(d),
             out_shape=(
@@ -1053,36 +1146,32 @@
                 jax.ShapeDtypeStruct((d.rows, D), BF),
                 jax.ShapeDtypeStruct((d.small, D), F32),
             ),
-            in_specs=[hbm, hbm, hbm, hbm, vmem] + [hbm] * len(d.w),
+            in_specs=[hbm, hbm, hbm, vmem, smem, smem, vmem] + [hbm] * len(d.w),
             out_specs=(hbm, hbm, hbm, hbm, vmem),
             scratch_shapes=[pltpu.VMEM(shape, dtype) for _, shape, dtype in scratch_list(d)]
             + [pltpu.SemaphoreType.DMA((SEMS,))] * 3,
             compiler_params=pltpu.CompilerParams(collective_id=0, has_side_effects=True, vmem_limit_bytes=63 << 20),
-        )(x_in, enc_in, cotangent, aux, gains_f, *[ws[name] for name in d.w])
+        )(x_in, enc_in, cotangent, jnp.transpose(table), dec_len, enc_len, gains, *[ws[name] for name in d.w])
         lo, ig, eg, gw, sm = outs
         others = d.ndp // (2 * d.nd)
         if others > 1:
             gw, sm = lax.psum((gw.astype(F32), sm), "dp")
             gw, sm = gw * (1.0 / (2 * d.nd)), sm * (1.0 / (2 * d.nd))
-        g = {name: gw[first : first + rows].astype(F32) for name, (first, rows) in d.w.items()}
-        mine = lax.dynamic_slice_in_dim(sm, 3 + lax.axis_index("mp") * nh, nh, axis=0)
-        col = jnp.arange(D)
-        dist = jnp.where(col < R, col, jnp.where(col < 3 * R - 1, col - R + 1, 4 * R))
-        pick = (bucket_index(dist)[:, None] == jnp.arange(NB)[None, :]).astype(F32)
-        table_grad = jnp.einsum("hl,lv->vh", mine, pick, precision=lax.Precision.HIGHEST, preferred_element_type=F32)
+        res = unpack(d, gw, lo, ig, eg, sm)
+        gu = jnp.transpose(res[3].reshape(D, F // 128, 2, 128), (0, 2, 1, 3)).reshape(D, 2, F)
         return (
-            lo,
-            ig.astype(F32),
-            eg.astype(F32),
-            jnp.transpose(g["qkv"].reshape(3, hc, D), (2, 0, 1)),
-            g["so"],
-            jnp.transpose(g["cq"]),
-            jnp.transpose(g["ckv"].reshape(2, hc, D), (2, 0, 1)),
-            g["co"],
-            jnp.transpose(g["gu"].reshape(2, F, D), (2, 0, 1)),
-            g["fo"],
-            sm[:3],
-            table_grad,
+            res[0],
+            res[1],
+            res[2],
+            jnp.transpose(res[5].reshape(3, hc, D), (2, 0, 1)),
+            res[6],
+            jnp.transpose(res[8]),
+            jnp.transpose(res[7].reshape(2, hc, D), (2, 0, 1)),
+            res[9],
+            gu,
+            res[4],
+            res[10],
+            jnp.transpose(res[11]),
         )
 
     return local

time: 237 us -> 212 us (0.89)
  other arithmetic: 11.6 us -> 0 us
  local copies, waits for them, and re-layouts: 11.5 us -> 0 us
  matrix products: 2.72 us -> 0 us
    pallas_call x1, Pallas kernels: 208 us -> 199 us  [local(): pl.pallas_call(build_kernel(d), out_shape=(jax.ShapeDtypeStruct((R, D), B...]
    convert_element_type x6 -> x0, other arithmetic: 8.43 us -> none  [the longest x2 2.49 us: local(): gw[first:first + rows].astype(F32)]
    transpose x2 -> x0, local copies, waits for them, and re-layouts: 8.03 us -> none  [the longest x1 4.87 us: local(): jnp.transpose(ff_in, (1, 2, 0)).reshape(2 * F, D)]
    pallas_call x0 -> x1, Pallas kernels: none -> 7.67 us  [unpack(): pl.pallas_call(kernel, grid=(steps,), in_specs=[pl.BlockSpec((2 * F, cols...]
    dot_general x2 -> x0, matrix products: 2.72 us -> none  [the longest x1 1.72 us: local(): jnp.einsum('hl,lv->vh', mine, pick, precision=lax.Precision.HIGHEST, pref...]
    slice x4 -> x0, local copies, waits for them, and re-layouts: 2.6 us -> none  [the longest x1 1.34 us: local(): sm[:3]]
    transpose x2 -> x0, other arithmetic: 2.44 us -> none  [the longest x1 1.35 us: local(): jnp.transpose(g['qkv'].reshape(3, hc, D), (2, 0, 1))]
where the time goes in v3:
time: 212 us; the launch traced here: 209 us
  Pallas kernels  207 us (98%)
  between operations  2.12 us (1%)
    pallas_call x1, Pallas kernels, local(): pl.pallas_call(build_kernel(d), out_shape=(jax.ShapeDtypeStruct((R, D), B...  199 us
    pallas_call x1, Pallas kernels, unpack(): pl.pallas_call(kernel, grid=(steps,), in_specs=[pl.BlockSpec((2 * F, cols...  7.67 us

profile of v3, /device:TPU:0, one launch (start us, length us, event | category | flops | bytes accessed | tf_op | source)
XLA Modules:
  0.0 209.2 jit_solution(10538579159279516764)
XLA Ops:
  1.9 199.4 %shard_map.229 = (bf16[256,768]{1,0:T(8,128)(2,1)}, bf16[256,768]{1,0:T(8,128)(2,1)}, bf16[128,768]{1,0:T(8,128)(2,1)}, bf16[3072,768]{1,0:T(8,128)(2,1)}, f32[16,768]{1,0:T(8,128)}) custom-call(bf16[256,768]{1,0:T(8,128)(2,1)} %refs_0_.1, bf16[128,768]{1,0:T(8,128)(2,1)} %refs_1_.1, bf16[256,768]{1,0:T(8,128)(2,1)} %refs_2_.1, bf16[3,32]{1,0:T(4,128)(2,1)} %bitcast.30, ...), custom_call_target="tpu_custom_call" | custom-call | tf_op jit(solution)/shard_map/pallas_call | solution.py:1140
  201.3 7.7 %shard_map.230 = (bf16[256,768]{1,0:T(8,128)(2,1)}, f32[256,768]{1,0:T(8,128)}, f32[128,768]{1,0:T(8,128)}, f32[6144,128]{1,0:T(8,128)}, f32[512,768]{1,0:T(8,12...) custom-call(bf16[3072,768]{1,0:T(8,128)(2,1)} %get-tuple-element.29., ...), custom_call_target="tpu_custom_call" | custom-call | tf_op jit(solution)/shard_map/pallas_call | solution.py:1100

commit v4 on v3

--- a/solution.py
+++ b/solution.py
@@ -88,7 +88,7 @@
         land += rows // d.nd
     d.land = land
     d.locrows = max(s, c, 2 * F)
-    d.small = -(-(3 + 4 * d.nh) // 8) * 8
+    d.small = -(-(3 + d.nh) // 8) * 8
     return d
 
 
@@ -583,8 +583,8 @@
         onehot = jnp.where(lax.broadcasted_iota(jnp.int32, (NB, 4 * R), 0) == bucket_index(dist), 1.0, 0.0).astype(BF)
         lines = dot_nn(tab_ref[...], onehot)
         v.aux0[...] = jnp.zeros(v.aux0.shape, F32)
-        v.aux0[pl.ds(0, 1)] = jnp.where(pos < dlen_ref[0], 0.0, MASK_FILL)
-        v.aux0[pl.ds(1, 1)] = jnp.where(pos < elen_ref[0], 0.0, MASK_FILL)
+        v.aux0[pl.ds(0, 1)] = jnp.where(pos < dlen_ref[...], 0.0, MASK_FILL)
+        v.aux0[pl.ds(1, 1)] = jnp.where(pos < elen_ref[...], 0.0, MASK_FILL)
         v.aux0[pl.ds(2, nh)] = jnp.where((pos >= R) & (pos < 2 * R), MASK_FILL, lines)
         v.aux0[pl.ds(2 + nh, nh)] = jnp.broadcast_to(lines[:, 2 * R : 2 * R + 1], (nh, 4 * R))
         saux.start()
@@ -927,7 +927,7 @@
         for h in range(2):
             rso.finish(h, fin_out)
         rs4.finish(1, fin4)
-        redG.combine()
+
 
         v.dka[...] = jnp.zeros(v.dka.shape, F32)
         v.dva[...] = jnp.zeros(v.dva.shape, F32)
@@ -936,9 +936,10 @@
         def self_back(k, carry):
             b = blk_ag(k)
             agd1.arrive(k)
+            pl.when(k == 1)(redG.combine)
+            pl.when(k == 3)(rse.kick)
             pl.when(k == 2)(out_lo.start)
-            pl.when(k == 3)(rse.kick)
-            pl.when(k == 2)(redH.combine)
+            pl.when(k == 3)(redH.combine)
 
             @pl.when(k == 3)
             def _():
@@ -989,8 +990,7 @@
             far = jnp.sum(jnp.sum(v.dsacc[h, 2], axis=0, keepdims=True), axis=1, keepdims=True)
             off = off + jnp.where(lane == 2 * R - 1, far, 0.0)
             line = jnp.concatenate([pltpu.roll(near, R + 1, 1)[:, :R], off], axis=1)
-            for q in range(4):
-                v.smc[pl.ds(3 + q * nh + h, 1), pl.ds(0, 3 * R)] = jnp.where(t == q, line, 0.0)
+            v.smc[pl.ds(3 + h, 1), pl.ds(0, 3 * R)] = line
 
         def fin5(h, rows, total):
             grad, part = norm_bwd(v.xb[rows].astype(F32), gain(0), total)
@@ -998,47 +998,49 @@
             v.igv[rows] = (v.gb[rows] + grad).astype(BF)
 
         plane = peers[1:]
-        lines = [zp, z2]
-        first = [Xfer(v.sms.at[i], v.smr.at[i], dev) for i, dev in enumerate(lines)]
-        second = [Xfer(v.sms.at[2], v.smr.at[3 + i], dev) for i, dev in enumerate(plane)]
-        third = [Xfer(v.sms.at[3], v.smr.at[6], sib)]
+        first = [Xfer(v.sms.at[0], v.smr.at[i], dev) for i, dev in enumerate(plane)]
+        rest = [Xfer(v.sms.at[1 + i], v.smr.at[3 + i], dev) for i, dev in enumerate([z2, zp, sib])]
         redS.combine()
         for h in range(2):
             rs5.finish(h, fin5)
         v.sms[0] = v.smc[...]
-        first[0].start()
-        first[0].recv()
-        v.sms[1] = v.sms[0] + v.smr[0]
-        first[1].start()
+        for x in first:
+            x.start()
         for x in out_ig:
             x.start()
         redS.finish()
+        for x in first:
+            x.recv()
+        if len(plane) == 3:
+            v.sms[1] = (v.sms[0] + v.smr[0]) + (v.smr[1] + v.smr[2])
+        elif len(plane) == 1:
+            v.sms[1] = v.sms[0] + v.smr[0]
+        else:
+            v.sms[1] = v.sms[0]
+        rest[0].start()
         redC.finish()
         redO.finish()
-        first[1].recv()
-        v.sms[2] = v.sms[1] + v.smr[1]
-        for x in second:
-            x.start()
+        rest[0].recv()
+        v.sms[2] = v.sms[1] + v.smr[3]
+        v.smc[...] = v.sms[2]
+        rest[1].start()
         rse.finish(0, fin_enc)
         out_eg.start()
         redG.relay()
         redH.relay()
+        rest[1].recv()
+        only = lax.broadcasted_iota(jnp.int32, v.smc.shape, 0) < 3
+        v.sms[3] = jnp.where(only, v.sms[2] + v.smr[4], v.sms[2])
+        rest[2].start()
         redC.relay()
-        for x in second:
-            x.recv()
-        if len(plane) == 3:
-            v.sms[3] = (v.sms[2] + v.smr[3]) + (v.smr[4] + v.smr[5])
-        elif len(plane) == 1:
-            v.sms[3] = v.sms[2] + v.smr[3]
-        else:
-            v.sms[3] = v.sms[2]
-        third[0].start()
         redO.relay()
         redS.relay()
-        third[0].recv()
-        sm_ref[...] = v.sms[3] + v.smr[6]
-
-        for x in first + second + third:
+        rest[2].recv()
+        total = v.sms[3] + v.smr[5]
+        table_rows = jnp.where(is_sw, v.smr[5], v.smc[...])
+        sm_ref[...] = jnp.where(only, total, table_rows)
+
+        for x in first + rest:
             x.sent()
         for x in (ag1, ag2, ag3, agd1, agd2, agd3, agenc, rs5, rso, rse):
             x.sent()
@@ -1081,10 +1083,7 @@
             col = lax.broadcasted_iota(jnp.int32, (1, D), 1)
             dist = jnp.where(col < R, col, jnp.where(col < 3 * R - 1, col - R + 1, 4 * R))
             pick = (lax.broadcasted_iota(jnp.int32, (NB, D), 0) == bucket_index(dist)).astype(F32)
-            z = lax.axis_index("mp")
-            mine = jnp.zeros((nh, D), F32)
-            for q in range(4):
-                mine = jnp.where(z == q, sm_ref[pl.ds(3 + q * nh, nh)], mine)
+            mine = sm_ref[pl.ds(3, nh)]
             table_out[...] = lax.dot_general(
                 mine, pick, (((1,), (1,)), ((), ())), precision=lax.Precision.HIGHEST, preferred_element_type=F32
             )
@@ -1127,7 +1126,6 @@
         R, D, hc, nh, F = d.R, d.D, d.hc, d.nh, d.F
         hbm = pl.BlockSpec(memory_space=pl.ANY)
         vmem = pl.BlockSpec(memory_space=pltpu.VMEM)
-        smem = pl.BlockSpec(memory_space=pltpu.SMEM)
         ws = {
             "qkv": jnp.transpose(self_qkv, (1, 2, 0)).reshape(3 * hc, D),
             "so": self_out,
@@ -1146,12 +1144,12 @@
                 jax.ShapeDtypeStruct((d.rows, D), BF),
                 jax.ShapeDtypeStruct((d.small, D), F32),
             ),
-            in_specs=[hbm, hbm, hbm, vmem, smem, smem, vmem] + [hbm] * len(d.w),
+            in_specs=[hbm, hbm, hbm, vmem, vmem, vmem, vmem] + [hbm] * len(d.w),
             out_specs=(hbm, hbm, hbm, hbm, vmem),
             scratch_shapes=[pltpu.VMEM(shape, dtype) for _, shape, dtype in scratch_list(d)]
             + [pltpu.SemaphoreType.DMA((SEMS,))] * 3,
             compiler_params=pltpu.CompilerParams(collective_id=0, has_side_effects=True, vmem_limit_bytes=63 << 20),
-        )(x_in, enc_in, cotangent, jnp.transpose(table), dec_len, enc_len, gains, *[ws[name] for name in d.w])
+        )(x_in, enc_in, cotangent, jnp.transpose(table), dec_len.reshape(1, 1), enc_len.reshape(1, 1), gains, *[ws[name] for name in d.w])
         lo, ig, eg, gw, sm = outs
         others = d.ndp // (2 * d.nd)
         if others > 1:

time: 212 us -> 208 us (0.981); the launches traced: 209 us -> 207 us
  no operation moved by 1% of the time
where the time goes in v4:
time: 208 us; the launch traced here: 207 us
  Pallas kernels  205 us (99%)
  between operations  2.12 us (1%)
    pallas_call x1, Pallas kernels, local(): pl.pallas_call(build_kernel(d), out_shape=(jax.ShapeDtypeStruct((R, D), B...  198 us
    pallas_call x1, Pallas kernels, unpack(): pl.pallas_call(kernel, grid=(steps,), in_specs=[pl.BlockSpec((2 * F, cols...  7.66 us

profile of v4, /device:TPU:0, one launch (start us, length us, event | category | flops | bytes accessed | tf_op | source)
XLA Modules:
  0.0 207.4 jit_solution(17872815803333709090)
XLA Ops:
  1.9 197.6 %shard_map.229 = (bf16[256,768]{1,0:T(8,128)(2,1)}, bf16[256,768]{1,0:T(8,128)(2,1)}, bf16[128,768]{1,0:T(8,128)(2,1)}, bf16[3072,768]{1,0:T(8,128)(2,1)}, f32[8,768]{1,0:T(8,128)}) custom-call(bf16[256,768]{1,0:T(8,128)(2,1)} %refs_0_.1, bf16[128,768]{1,0:T(8,128)(2,1)} %refs_1_.1, bf16[256,768]{1,0:T(8,128)(2,1)} %refs_2_.1, bf16[3,32]{1,0:T(4,128)(2,1)} %bitcast.34, ...), custom_call_target="tpu_custom_call" | custom-call | tf_op jit(solution)/shard_map/pallas_call | solution.py:1138
  199.5 7.7 %shard_map.230 = (bf16[256,768]{1,0:T(8,128)(2,1)}, f32[256,768]{1,0:T(8,128)}, f32[128,768]{1,0:T(8,128)}, f32[6144,128]{1,0:T(8,128)}, f32[512,768]{1,0:T(8,12...) custom-call(bf16[3072,768]{1,0:T(8,128)(2,1)} %get-tuple-element.29., ...), custom_call_target="tpu_custom_call" | custom-call | tf_op jit(solution)/shard_map/pallas_call | solution.py:1099

commit v5 on v4

--- a/solution.py
+++ b/solution.py
@@ -773,8 +773,7 @@
 
         for h in range(2):
             rs1.finish(h, fin1)
-        for name in ("gu", "fo"):
-            weights[name].start()
+        weights["gu"].start()
 
         weights["cq"].wait()
         weights["co"].wait()
@@ -787,6 +786,7 @@
 
         def send_cot(h):
             pl.when(h == 0)(scot.wait)
+            pl.when(h == 0)(weights["fo"].start)
             rows = pl.ds(pl.multiple_of(h * HR, HR), HR)
             v.d3f[h, a, pl.ds(pl.multiple_of(c * HR, HR), HR)] = v.cotb[rows]
             agd3.send(h)

time: 208 us -> 211 us (1.014)
  Pallas kernels: 205 us -> 208 us
    pallas_call x1, Pallas kernels: 198 us -> 200 us  [local(): pl.pallas_call(build_kernel(d), out_shape=(jax.ShapeDtypeStruct((R, D), B...]
where the time goes in v5:
time: 211 us; the launch traced here: 210 us
  Pallas kernels  208 us (99%)
  between operations  2.12 us (1%)
    pallas_call x1, Pallas kernels, local(): pl.pallas_call(build_kernel(d), out_shape=(jax.ShapeDtypeStruct((R, D), B...  200 us
    pallas_call x1, Pallas kernels, unpack(): pl.pallas_call(kernel, grid=(steps,), in_specs=[pl.BlockSpec((2 * F, cols...  7.66 us

profile of v5, /device:TPU:0, one launch (start us, length us, event | category | flops | bytes accessed | tf_op | source)
XLA Modules:
  0.0 210.2 jit_solution(5175956393515995618)
XLA Ops:
  1.9 200.4 %shard_map.229 = (bf16[256,768]{1,0:T(8,128)(2,1)}, bf16[256,768]{1,0:T(8,128)(2,1)}, bf16[128,768]{1,0:T(8,128)(2,1)}, bf16[3072,768]{1,0:T(8,128)(2,1)}, f32[8,768]{1,0:T(8,128)}) custom-call(bf16[256,768]{1,0:T(8,128)(2,1)} %refs_0_.1, bf16[128,768]{1,0:T(8,128)(2,1)} %refs_1_.1, bf16[256,768]{1,0:T(8,128)(2,1)} %refs_2_.1, bf16[3,32]{1,0:T(4,128)(2,1)} %bitcast.34, ...), custom_call_target="tpu_custom_call" | custom-call | tf_op jit(solution)/shard_map/pallas_call | solution.py:1138
  202.3 7.7 %shard_map.230 = (bf16[256,768]{1,0:T(8,128)(2,1)}, f32[256,768]{1,0:T(8,128)}, f32[128,768]{1,0:T(8,128)}, f32[6144,128]{1,0:T(8,128)}, f32[512,768]{1,0:T(8,12...) custom-call(bf16[3072,768]{1,0:T(8,128)(2,1)} %get-tuple-element.29., ...), custom_call_target="tpu_custom_call" | custom-call | tf_op jit(solution)/shard_map/pallas_call | solution.py:1099
